TPU v7x, 256 devices: a whole 4x4x8 slice. The times are simulated.
256 devices in a mesh: gx: 32 (over y, z_hi, x), gy: 8 (over z_lo, core).
Axes of the slice: x: 4, y: 4, z: 8 (z_hi: 2, z_lo: 4; z = z_hi * 4 + z_lo), core: 2. Of those that a mesh axis runs over, the one named last changes fastest.
Arguments:
- fluid_position: float32 [3, 32, 8, 4096], P(None, 'gx', 'gy'), may hold values from 0 to 1
- fluid_velocity: float32 [3, 32, 8, 4096], P(None, 'gx', 'gy'), may hold values from -6 to 6
- fluid_mass: float32 [32, 8, 4096], P('gx', 'gy'), may hold values from 0.5 to 2
- fluid_counts: int32 [32, 8, 32], P('gx', 'gy'), may hold values from 1 to 128
- fluid_lists: int32 [32, 8, 32, 8], P('gx', 'gy'), may hold values from 0 to 287, as said below
- coupling_lists: int32 [32, 8, 32, 4], P('gx', 'gy'), may hold values from 0 to 143
- boulder_position: float32 [3, 32, 8, 2048], P(None, 'gx', 'gy'), may hold values from 0 to 1, as said below
- boulder_velocity: float32 [3, 32, 8, 2048], P(None, 'gx', 'gy'), may hold values from -6 to 6
- boulder_radius: float32 [32, 8, 2048], P('gx', 'gy'), may hold values from 0.03 to 0.07
- boulder_mass: float32 [32, 8, 2048], P('gx', 'gy'), may hold values from 0.5 to 2
- boulder_counts: int32 [32, 8, 16], P('gx', 'gy'), may hold values from 1 to 128
- contact_ids: int32 [32, 8, 8, 2048], P('gx', 'gy'), may hold values from 0 to 18431, as said below
- spring_history: float32 [3, 32, 8, 8, 2048], P(None, 'gx', 'gy'), may hold values from -0.3 to 0.3
Outputs:
- fluid_accel: float32 [3, 32, 8, 4096], P(None, 'gx', 'gy')
- fluid_density: float32 [32, 8, 4096], P('gx', 'gy')
- boulder_accel: float32 [3, 32, 8, 2048], P(None, 'gx', 'gy')
- history_out: float32 [3, 32, 8, 8, 2048], P(None, 'gx', 'gy')
Inputs may be any that keep to these rules, and one draw needn't show every extreme that they name: `fluid_lists`: entry n names block n % 32 of the tile offset by n // 96 - 1 along gx and n // 32 % 3 - 1 along gy, periodically; never the listing block itself; repeats may occur. `coupling_lists`: entry n names boulder block n % 16 of the tile offset by n // 48 - 1 along gx and n // 16 % 3 - 1 along gy, periodically; repeats may occur. `contact_ids`: entry n names boulder n % 2048 of the tile offset by n // 6144 - 1 along gx and n // 2048 % 3 - 1 along gy, periodically; partners are nearby boulders of the same or an adjacent tile; never the boulder itself; partners may be dead slots. `boulder_position`: x and y lie in [0, 1); z is nonnegative.
All inputs are finite; a program needn't handle non-finite values.
Results may differ from a plain program's by a relative error of at most 0.0003.
Values sent between devices are 32-bit elements; how exact they have to be, the bound alone decides.
A program may use at most 64 MiB of HBM per device.

v0:
```python
import jax
import jax.numpy as jnp
from jax import lax
from jax.experimental import pallas as pl
from jax.experimental.pallas import tpu as pltpu
from jax.sharding import PartitionSpec as P

F32 = jnp.float32
BF16 = jnp.bfloat16
MESH = pl.DeviceIdType.MESH
NT = (((1,), (1,)), ((), ()))
NN = (((1,), (0,)), ((), ()))

INV_H2 = 1.0 / 0.3**2
REST = 10.0
STIFF = 10.0
COUPLE = 0.1
NORMAL_K = 10.0
SHEAR_K = 20.0
DT = 0.05
SOFT2 = 0.02**2
PRESS_C = 6.0 / 0.3**2


def rounded(x):
    return x.astype(BF16).astype(F32)


def split3(x):
    hi = rounded(x)
    rest = x - hi
    mid = rounded(rest)
    return hi, mid, rest - mid


def dot(a, b, dims):
    return lax.dot_general(a, b, dims, preferred_element_type=F32)


def left_stack(x):
    h, m, l = split3(x)
    return jnp.concatenate([h, h, m, m, h, l], axis=0)


def right_stack(x):
    h, m, l = split3(x)
    return jnp.concatenate([h, m, h, m, l, h], axis=0).astype(BF16)


def stack3(x):
    return jnp.concatenate(split3(x), axis=0).astype(BF16)


def sum3(x):
    return x[0:8] + x[8:16] + x[16:24]


def row8(x):
    return jnp.broadcast_to(x, (8, x.shape[-1]))


def halves(x):
    hi = x.astype(BF16)
    return hi, (x - hi.astype(F32)).astype(BF16)


def tile_offsets(tile):
    third = (tile * 11) >> 5
    return (third - 1).astype(F32), (tile - 3 * third - 1).astype(F32)


def kernel(
    fl, cl, fcnt, bcnt,
    fpos, fvel, fmass, clv, bpos, bvel, brad, bmass,
    o_fa, o_fd, hb, o_cp,
    hf, hd, ut, qh, ql, fx, fu, fi, sp, cp, ry, red, rx,
    cnf, cnb, dens, dr, pf, ssem, rsem,
    *, n_x, n_y,
):
    me_x = lax.axis_index("gx")
    me_y = lax.axis_index("gy")
    xp = (lax.rem(me_x + 1, n_x), me_y)
    xm = (lax.rem(me_x + n_x - 1, n_x), me_y)
    yp = (me_x, lax.rem(me_y + 1, n_y))
    ym = (me_x, lax.rem(me_y + n_y - 1, n_y))

    barrier = pltpu.get_barrier_semaphore()
    for dev in (xp, xm, yp, ym):
        pl.semaphore_signal(barrier, inc=1, device_id=dev, device_id_type=MESH)

    row = lax.broadcasted_iota(jnp.int32, (8, 128), 0)
    lane = lax.broadcasted_iota(jnp.int32, (32, 128), 1)

    for b in range(32):
        cnf[b : b + 1, :] = jnp.full((1, 128), fcnt[b], jnp.int32)
    for b in range(16):
        cnb[b : b + 1, :] = jnp.full((1, 128), bcnt[b], jnp.int32)
    f_on = lane < cnf[...]
    b_on = lane[:16] < cnb[...]
    croot = jnp.where(f_on, jnp.exp(jnp.log(fmass[...]) * (1.0 / 3.0)), 0.0)
    for b in range(32):
        s = slice(b, b + 1)
        hf[128 + b] = jnp.concatenate(
            [croot[s], fpos[0, s, :], fpos[1, s, :], fpos[2, s, :]], axis=0
        )
    bm_live = jnp.where(b_on, bmass[...], 0.0)
    for b in range(16):
        s = slice(b, b + 1)
        hb[64 + b] = jnp.concatenate(
            [bm_live[s]]
            + [bpos[d, s, :] for d in range(3)]
            + [bvel[d, s, :] for d in range(3)]
            + [brad[s, :]],
            axis=0,
        )

    def copy(src, dst, k, dev):
        return pltpu.make_async_remote_copy(
            src_ref=src, dst_ref=dst, send_sem=ssem.at[k], recv_sem=rsem.at[k],
            device_id=dev, device_id_type=MESH,
        )

    def halo(ref, width, base):
        at = lambda t: ref.at[pl.ds(t * width, width)]
        return {
            1: copy(at(4), at(1), base + 0, xp),
            7: copy(at(4), at(7), base + 1, xm),
            3: copy(at(4), at(3), base + 2, yp),
            5: copy(at(4), at(5), base + 3, ym),
            0: copy(at(1), at(0), base + 4, yp),
            2: copy(at(1), at(2), base + 5, ym),
            6: copy(at(7), at(6), base + 6, yp),
            8: copy(at(7), at(8), base + 7, ym),
        }

    cf = halo(hf, 32, 0)
    cb = halo(hb, 16, 8)
    cd = halo(hd, 32, 16)
    c_yp = copy(cp.at[2], ry.at[0], 24, yp)
    c_ym = copy(cp.at[0], ry.at[1], 25, ym)
    c_xp = copy(red.at[2], rx.at[0], 26, xp)
    c_xm = copy(red.at[0], rx.at[1], 27, xm)

    pl.semaphore_wait(barrier, 4)
    for k in (1, 7, 3, 5):
        cf[k].start()
    for k in (1, 7, 3, 5):
        cb[k].start()

    u_planes = [fvel[d] for d in range(3)]
    mf_live = jnp.where(f_on, fmass[...], 0.0)
    one1 = jnp.ones((1, 128), F32)
    zero3 = jnp.zeros((3, 128), F32)
    for b in range(32):
        s = slice(b, b + 1)
        v = jnp.concatenate(
            [one1, zero3, u_planes[0][s], u_planes[1][s], u_planes[2][s], zero3[:1]], axis=0
        )
        fu[b] = v
        fi[b] = v * row8(mf_live[s])

    zeros80 = jnp.zeros((80, 128), F32)

    def own_left(i, _):
        raw = hf[128 + i]
        x = raw - 0.5
        x1, x2, x3 = x[1:2], x[2:3], x[3:4]
        norm = -(x1 * x1 + x2 * x2 + x3 * x3)
        u8 = jnp.concatenate([norm, x1, x2, x3, one1, zero3], axis=0)
        full = jnp.concatenate([left_stack(u8), zeros80], axis=0)
        ut[i] = full.T.astype(BF16)
        return 0

    lax.fori_loop(0, 32, own_left, 0)


    for k in (1, 7):
        cf[k].wait_recv()
    for k in (0, 2, 6, 8):
        cf[k].start()
    for k in (1, 7):
        cb[k].wait_recv()
    for k in (0, 2, 6, 8):
        cb[k].start()
    for k in (3, 5, 0, 2, 6, 8):
        cf[k].wait_recv()

    coord = (row >= 1) & (row <= 3)
    fac = jnp.where(row == 0, INV_H2, 2.0 * INV_H2)
    ones8 = jnp.ones((8, 128), BF16)
    zeros4 = jnp.zeros((4, 128), F32)

    def density(i, _):
        lhs = ut[i][:, 0:48]
        acc = jnp.zeros((128, 128), F32)
        for jj in range(4):
            cols = []
            for h in range(2):
                j = jj * 2 + h
                nid = fl[i * 8 + j]
                ox, oy = tile_offsets(nid >> 5)
                raw = jnp.concatenate([hf[nid], zeros4], axis=0)
                shift = jnp.where(
                    row == 1, ox - 0.5, jnp.where(row == 2, oy - 0.5, -0.5)
                )
                x = jnp.where(coord, raw + shift, 0.0)
                c8 = row8(raw[0:1])
                n8 = jnp.sum(x * x, axis=0, keepdims=True)
                y = jnp.where(row == 0, c8, c8 * x)
                fx[i * 8 + j] = y
                w = jnp.where(row < 4, y * fac, jnp.where(row == 4, c8 * (1.0 - INV_H2 * n8), 0.0))
                cols.append(right_stack(w))
            u = jnp.maximum(dot(lhs, jnp.concatenate(cols, axis=1), NN), 0.0)
            sq = u * u
            cube = sq * u
            acc = acc + (cube[:, 0:128] + cube[:, 128:256])
            hi, lo = halves(sq)
            qh[i, :, jj * 256 : (jj + 1) * 256] = hi
            ql[i, :, jj * 256 : (jj + 1) * 256] = lo
        a, b, c = split3(acc)
        total = (
            dot(ones8, a.astype(BF16), NT)
            + dot(ones8, b.astype(BF16), NT)
            + dot(ones8, c.astype(BF16), NT)
        )
        dens[pl.ds(i, 1), :] = total[0:1]
        return 0

    lax.fori_loop(0, 32, density, 0)
    rho = fmass[...] + dens[...]
    weight = STIFF * (rho / REST - 1.0) / (rho * rho)
    for b in range(32):
        hd[128 + b] = weight[b : b + 1]
    for k in (1, 7, 3, 5):
        cd[k].start()
    o_fd[...] = jnp.where(f_on, rho, 0.0)

    for k in (3, 5, 0, 2, 6, 8):
        cb[k].wait_recv()
    fac2 = jnp.where(row == 0, 1.0, 2.0)

    def coupling(i, _):
        lhs = ut[i][:, 0:48]
        cols = []
        funs = []
        for j in range(4):
            nid = cl[i * 4 + j]
            ox, oy = tile_offsets(nid >> 4)
            raw = hb[nid]
            shift = jnp.where(row == 1, ox - 0.5, jnp.where(row == 2, oy - 0.5, -0.5))
            x = jnp.where(coord, raw + shift, 0.0)
            m8 = row8(raw[0:1])
            c8 = jnp.where(m8 > 0.0, jnp.sqrt(jnp.maximum(m8, 1e-30)), 0.0)
            reach = row8(raw[7:8]) + COUPLE
            t8 = 1.0 / (reach * reach)
            n8 = jnp.sum(x * x, axis=0, keepdims=True)
            y = jnp.where(row == 0, c8, c8 * x)
            w = jnp.where(row < 4, y * (t8 * fac2), jnp.where(row == 4, c8 * (1.0 - t8 * n8), 0.0))
            cols.append(right_stack(w))
            funs.append(stack3(jnp.where(row == 0, 1.0, raw)))
        fside = stack3(fi[i])
        pulled = jnp.zeros((24, 128), F32)
        for h in range(2):
            rhs = jnp.concatenate(cols[2 * h : 2 * h + 2], axis=1)
            u = jnp.maximum(dot(lhs, rhs, NN), 0.0)
            hi, lo = halves(u * u)
            fun = jnp.concatenate(funs[2 * h : 2 * h + 2], axis=1)
            pulled = pulled + dot(fun, hi, NT) + dot(fun, lo, NT)
            back = sum3(dot(fside, hi, NN) + dot(fside, lo, NN))
            for g in range(2):
                at = pl.ds(pl.multiple_of((i * 4 + 2 * h + g) * 8, 8), 8)
                sp[at, :] = back[:, g * 128 : (g + 1) * 128]
        d8 = sum3(pulled)
        drag = d8 - fu[i] * row8(d8[0:1])
        for d in range(3):
            dr[d, pl.ds(i, 1), :] = drag[4 + d : 5 + d]
        return 0

    lax.fori_loop(0, 32, coupling, 0)

    for k in (1, 7):
        cd[k].wait_recv()
    for k in (0, 2, 6, 8):
        cd[k].start()

    onehot = (
        lax.broadcasted_iota(jnp.int32, (144, 128), 0) == jnp.broadcast_to(clv[...], (144, 128))
    ).astype(F32).astype(BF16)

    def reduced(r):
        parts = split3(sp[pl.ds(r, 128, stride=8), :])
        m = jnp.concatenate([v.astype(BF16) for v in parts], axis=1)
        got = dot(onehot, m, NN)
        return got[:, 0:128] + got[:, 128:256] + got[:, 256:384]

    mass_sum = reduced(0)
    for d in range(3):
        vel = hb[:, 4 + d, :]
        part = reduced(4 + d) - vel * mass_sum
        for t in range(9):
            cp[t % 3, t // 3, d] = part[t * 16 : (t + 1) * 16]
    c_yp.start()
    c_ym.start()

    c_yp.wait_recv()
    c_ym.wait_recv()
    for g in range(3):
        red[g] = cp[1, g] + (ry[0, g] + ry[1, g])
    c_xp.start()
    c_xm.start()

    for k in (3, 5, 0, 2, 6, 8):
        cd[k].wait_recv()

    def pressure(i, _):
        got = jnp.zeros((24, 128), F32)
        for j in range(8):
            nid = fl[i * 8 + j]
            y = fx[i * 8 + j]
            w8 = row8(hd[nid])
            fun = stack3(jnp.concatenate([y[0:4], (y * w8)[0:4]], axis=0))
            at = slice(j * 128, (j + 1) * 128)
            got = got + dot(fun, qh[i, :, at], NT) + dot(fun, ql[i, :, at], NT)
        p8 = sum3(got)
        w_i = row8(hd[128 + i])
        comb = w_i[0:4] * p8[0:4] + p8[4:8]
        x = hf[128 + i] - 0.5
        force = x * jnp.broadcast_to(comb[0:1], (4, 128)) - comb
        for d in range(3):
            pf[d, pl.ds(i, 1), :] = force[d + 1 : d + 2]
        return 0

    lax.fori_loop(0, 32, pressure, 0)
    for d in range(3):
        down = -1.0 if d == 2 else 0.0
        o_fa[d] = jnp.where(f_on, PRESS_C * pf[d] + dr[d] + down, 0.0)

    c_xp.wait_recv()
    c_xm.wait_recv()
    for d in range(3):
        o_cp[d] = red[1, d] + (rx[0, d] + rx[1, d])

    for group in (cf, cb, cd):
        for k in group:
            group[k].wait_send()
    for c in (c_yp, c_ym, c_xp, c_xm):
        c.wait_send()


def contact_kernel(
    bcnt, bpos, bvel, brad, bmass, cid, hist, hb, coupled, o_ba, o_h, ga, cnb, pu
):
    for b in range(16):
        cnb[b : b + 1, :] = jnp.full((1, 128), bcnt[b], jnp.int32)

    def block(b, _):
        st = pl.multiple_of(b * 128, 128)
        ids8 = cid[:, pl.ds(st, 128)]
        for q in range(8):
            ids = row8(ids8[q : q + 1])
            ln = ids & 127
            bits = [(ids & (128 << k)) != 0 for k in range(4)]
            tl = ids >> 11
            out = None
            for t in range(9):
                vals = [
                    jnp.take_along_axis(
                        hb[t * 16 + r], ln, axis=1,
                        mode="promise_in_bounds",
                    )
                    for r in range(16)
                ]
                for k in range(4):
                    vals = [
                        jnp.where(bits[k], vals[j + 1], vals[j]) for j in range(0, len(vals), 2)
                    ]
                out = vals[0] if out is None else jnp.where(tl == t, vals[0], out)
            ga[q * 8 : q * 8 + 8, :] = out

        ox, oy = tile_offsets(ids8 >> 11)
        got = [ga[pl.ds(f, 8, stride=8), :] for f in range(8)]
        at = pl.ds(b, 1)
        r1 = row8(bpos[0, at, :]) - (got[1] + ox)
        r2 = row8(bpos[1, at, :]) - (got[2] + oy)
        r3 = row8(bpos[2, at, :]) - got[3]
        dist = jnp.sqrt((r1 * r1 + r2 * r2) + r3 * r3 + SOFT2)
        inv = 1.0 / dist
        nrm = (r1 * inv, r2 * inv, r3 * inv)
        inter = jnp.where(got[0] > 0.0, jnp.maximum(row8(brad[at, :]) + got[7] - dist, 0.0), 0.0)
        rel = [row8(bvel[d, at, :]) - got[4 + d] for d in range(3)]
        along = (rel[0] * nrm[0] + rel[1] * nrm[1]) + rel[2] * nrm[2]
        touch = jnp.minimum(inter * 100.0, 1.0)
        on = lax.broadcasted_iota(jnp.int32, (8, 128), 1) < jnp.broadcast_to(cnb[at, :], (8, 128))
        for d in range(3):
            spring = (hist[d, :, pl.ds(st, 128)] + DT * (rel[d] - along * nrm[d])) * touch
            push = NORMAL_K * inter * nrm[d] - SHEAR_K * spring
            pu[d, at, :] = jnp.sum(push, axis=0, keepdims=True)
            o_h[d, :, pl.ds(st, 128)] = jnp.where(on, spring, 0.0)
        return 0

    lax.fori_loop(0, 16, block, 0)
    b_on = lax.broadcasted_iota(jnp.int32, (16, 128), 1) < cnb[...]
    for d in range(3):
        down = -1.0 if d == 2 else 0.0
        o_ba[d] = jnp.where(b_on, (pu[d] + coupled[d]) / bmass[...] + down, 0.0)


def body(
    fluid_position, fluid_velocity, fluid_mass, fluid_counts, fluid_lists, coupling_lists,
    boulder_position, boulder_velocity, boulder_radius, boulder_mass, boulder_counts,
    contact_ids, spring_history,
):
    n_x, n_y = lax.axis_size("gx"), lax.axis_size("gy")
    vm = pl.BlockSpec(memory_space=pltpu.VMEM)
    sm = pl.BlockSpec(memory_space=pltpu.SMEM)
    counts_b = boulder_counts.reshape(16)
    pos_b = boulder_position.reshape(3, 16, 128)
    vel_b = boulder_velocity.reshape(3, 16, 128)
    rad_b = boulder_radius.reshape(16, 128)
    mass_b = boulder_mass.reshape(16, 128)
    fa, fd, hood, coupled = pl.pallas_call(
        lambda *refs: kernel(*refs, n_x=n_x, n_y=n_y),
        name="step",
        out_shape=(
            jax.ShapeDtypeStruct((3, 32, 128), F32),
            jax.ShapeDtypeStruct((32, 128), F32),
            jax.ShapeDtypeStruct((144, 8, 128), F32),
            jax.ShapeDtypeStruct((3, 16, 128), F32),
        ),
        in_specs=[sm] * 4 + [vm] * 8,
        out_specs=(vm,) * 4,
        scratch_shapes=[
            pltpu.VMEM((288, 4, 128), F32),
            pltpu.VMEM((288, 1, 128), F32),
            pltpu.VMEM((32, 128, 128), BF16),
            pltpu.VMEM((32, 128, 1024), BF16),
            pltpu.VMEM((32, 128, 1024), BF16),
            pltpu.VMEM((256, 8, 128), F32),
            pltpu.VMEM((32, 8, 128), F32),
            pltpu.VMEM((32, 8, 128), F32),
            pltpu.VMEM((1024, 128), F32),
            pltpu.VMEM((3, 3, 3, 16, 128), F32),
            pltpu.VMEM((2, 3, 3, 16, 128), F32),
            pltpu.VMEM((3, 3, 16, 128), F32),
            pltpu.VMEM((2, 3, 16, 128), F32),
            pltpu.VMEM((32, 128), jnp.int32),
            pltpu.VMEM((16, 128), jnp.int32),
            pltpu.VMEM((32, 128), F32),
            pltpu.VMEM((3, 32, 128), F32),
            pltpu.VMEM((3, 32, 128), F32),
            pltpu.SemaphoreType.DMA((28,)),
            pltpu.SemaphoreType.DMA((28,)),
        ],
        compiler_params=pltpu.CompilerParams(
            collective_id=0, has_side_effects=True, vmem_limit_bytes=48 * 1024 * 1024
        ),
    )(
        fluid_lists.reshape(256),
        coupling_lists.reshape(128),
        fluid_counts.reshape(32),
        counts_b,
        fluid_position.reshape(3, 32, 128),
        fluid_velocity.reshape(3, 32, 128),
        fluid_mass.reshape(32, 128),
        coupling_lists.reshape(1, 128),
        pos_b,
        vel_b,
        rad_b,
        mass_b,
    )
    ba, ho = pl.pallas_call(
        contact_kernel,
        name="contact",
        out_shape=(
            jax.ShapeDtypeStruct((3, 16, 128), F32),
            jax.ShapeDtypeStruct((3, 8, 2048), F32),
        ),
        in_specs=[sm] + [vm] * 8,
        out_specs=(vm,) * 2,
        scratch_shapes=[
            pltpu.VMEM((64, 128), F32),
            pltpu.VMEM((16, 128), jnp.int32),
            pltpu.VMEM((3, 16, 128), F32),
        ],
    )(
        counts_b, pos_b, vel_b, rad_b, mass_b,
        contact_ids.reshape(8, 2048), spring_history.reshape(3, 8, 2048), hood, coupled,
    )
    return (
        fa.reshape(3, 1, 1, 4096),
        fd.reshape(1, 1, 4096),
        ba.reshape(3, 1, 1, 2048),
        ho.reshape(3, 1, 1, 8, 2048),
    )


def solution(mesh):
    v4 = P(None, "gx", "gy", None)
    v3 = P("gx", "gy", None)
    l4 = P("gx", "gy", None, None)
    h5 = P(None, "gx", "gy", None, None)
    return jax.shard_map(
        body,
        mesh=mesh,
        in_specs=(v4, v4, v3, v3, l4, l4, v4, v4, v3, v3, v3, l4, h5),
        out_specs=(v4, v3, v4, h5),
        check_vma=False,
    )
```

profile of v0, /device:TPU:1, one launch (start us, length us, event | category | flops | bytes accessed | tf_op | source)
XLA Modules:
  0.0 105.5 jit_solution(1396763042171436681)
XLA Ops:
  0.6 0.0 copy-start.11
  0.6 0.0 copy-start.5
  0.7 0.0 copy-start.3
  0.7 0.7 copy-done.11
  1.3 0.1 copy.23
  1.4 0.1 reshape.69.refs_7_
  1.5 0.0 copy-start.1
  1.5 0.0 copy-start.2
  1.5 0.1 reshape.63.refs_1_
  1.6 0.8 copy.22
  2.4 0.0 copy-start.9
  2.4 0.0 copy-start.10
  2.4 0.1 reshape.62.refs_0_
  2.5 0.0 copy-done.5
  2.5 0.0 copy-done.3
  2.5 0.0 copy-done.1
  2.5 0.0 copy-done.2
  2.5 0.5 copy-done.9
  3.1 0.0 copy-done.10
  3.1 0.0 copy-start.4
  3.1 0.8 copy-done.4
  3.9 0.0 copy-start.6
  3.9 0.7 copy-done.6
  4.6 0.0 copy-start.8
  4.6 0.7 copy-done.8
  5.3 74.0 %step.1 = (f32[3,32,128]{2,1,0:T(8,128)S(1)}, f32[32,128]{1,0:T(8,128)S(1)}, f32[144,8,128]{2,1,0:T(8,128)S(1)}, f32[3,16,128]{2,1,0:T(8,128)S(1)}) custom-call(s32[256]{0:T(256)S(1)} %reshape.62.refs_0_, s32[128]{0:T(128)S(1)} %reshape.63.refs_1_, s32[32]{0:T(128)S(1)} %bitcast.38, s32[16]{0:T(128)S(1)} %bitcast.37, f32[3,32,128]{2,1,0:T(8,128)S(1)} %bitcast.28, ...), custom_call_target="tpu_custom_call" | custom-call | tf_op jit(solution)/shard_map/step/pallas_call | solution.py:421
  79.3 0.0 copy-start
  79.3 0.8 copy-done
  80.1 0.0 copy-start.7
  80.1 0.6 copy-done.7
  80.7 23.6 %contact.1 = (f32[3,16,128]{2,1,0:T(8,128)}, f32[3,8,2048]{2,1,0:T(8,128)}) custom-call(s32[16]{0:T(128)} %bitcast.36, f32[3,16,128]{2,1,0:T(8,128)} %bitcast.23, f32[3,16,128]{2,1,0:T(8,128)} %bitcast.25, f32[16,128]{1,0:T(8,128)} %bitcast.30, f32[16,128]{1,0:T(8,128)} %bitcast.32, s32[8,2048]{1,0:T(8,128)} %bitcast.40, f32[3,8,2048]{2,1,0:T(8,128)} %bitcast.39, ...), custom_call_target="tpu_custom_call" | custom-call | tf_op jit(solution)/shard_map/contact/pallas_call | solution.py:471
  104.3 0.6 copy.30
  104.9 0.6 copy.31
Async XLA Ops:
  0.6 0.7 copy-start.11
  0.6 1.9 %copy-start.5 = (f32[1,1,2048]{2,1,0:T(1,128)S(1)}, f32[1,1,2048]{2,1,0:T(1,128)}, u32[]{:S(2)}) copy-start(f32[1,1,2048]{2,1,0:T(1,128)} %param.21) | copy-start | bytes 24580
  0.7 1.9 %copy-start.3 = (f32[3,1,1,4096]{3,2,1,0:T(1,128)S(1)}, f32[3,1,1,4096]{3,2,1,0:T(1,128)}, u32[]{:S(2)}) copy-start(f32[3,1,1,4096]{3,2,1,0:T(1,128)} %param.13) | copy-start | bytes 147460
  1.5 1.0 copy-start.1
  1.5 1.0 copy-start.2
  2.4 0.7 copy-start.9
  2.4 0.7 copy-start.10
  3.1 0.8 copy-start.4
  3.9 0.7 copy-start.6
  4.6 0.7 copy-start.8
  79.3 0.8 copy-start
  80.1 0.6 copy-start.7
where the time goes:
time: 107 us; the launch traced here: 106 us
  Pallas kernels  97.6 us (91%)
  local copies, waits for them, and re-layouts  7.21 us (7%)
    pallas_call x1, Pallas kernels, body(): pl.pallas_call(lambda *refs: kernel(*refs, n_x=n_x, n_y=n_y), name='step'...  74 us
    pallas_call x1, Pallas kernels, body(): pl.pallas_call(contact_kernel, name='contact', out_shape=(jax.ShapeDtypeS...  23.6 us
    unnamed x28, local copies, waits for them, and re-layouts  6.92 us

commit v1 on v0

--- a/solution.py
+++ b/solution.py
@@ -71,10 +71,10 @@
 
 def kernel(
     fl, cl, fcnt, bcnt,
-    fpos, fvel, fmass, clv, bpos, bvel, brad, bmass,
-    o_fa, o_fd, hb, o_cp,
-    hf, hd, ut, qh, ql, fx, fu, fi, sp, cp, ry, red, rx,
-    cnf, cnb, dens, dr, pf, ssem, rsem,
+    fpos, fvel, fmass, clv, bpos, bvel, brad, bmass, cid, hist,
+    o_fa, o_fd, o_ba, o_h,
+    hf, hb, hd, ut, qh, ql, fx, fu, fi, ga, sp, cp, ry, red, rx,
+    cnf, cnb, dens, dr, pf, pu, ssem, rsem,
     *, n_x, n_y,
 ):
     me_x = lax.axis_index("gx")
@@ -173,6 +173,39 @@
 
     lax.fori_loop(0, 32, own_left, 0)
 
+    def gather(tiles, first):
+        def block(b, _):
+            st = pl.multiple_of(b * 128, 128)
+            ids8 = cid[:, pl.ds(st, 128)]
+            for q in range(8):
+                ids = row8(ids8[q : q + 1])
+                ln = ids & 127
+                bits = [(ids & (128 << k)) != 0 for k in range(4)]
+                tl = ids >> 11
+                at = pl.ds(pl.multiple_of(b * 64 + q * 8, 8), 8)
+                out = jnp.zeros((8, 128), F32) if first else ga[at, :]
+                for t in tiles:
+                    vals = [
+                        jnp.take_along_axis(
+                            hb[t * 16 + r], ln, axis=1,
+                            mode="promise_in_bounds",
+                        )
+                        for r in range(16)
+                    ]
+                    for k in range(4):
+                        vals = [
+                            jnp.where(bits[k], vals[j + 1], vals[j]) for j in range(0, len(vals), 2)
+                        ]
+                    out = jnp.where(tl == t, vals[0], out)
+                ga[at, :] = out
+            return 0
+
+        lax.fori_loop(0, 16, block, 0)
+
+    gather((4,), True)
+    cb[3].wait_recv()
+    cb[5].wait_recv()
+    gather((3, 5), False)
 
     for k in (1, 7):
         cf[k].wait_recv()
@@ -235,7 +268,7 @@
         cd[k].start()
     o_fd[...] = jnp.where(f_on, rho, 0.0)
 
-    for k in (3, 5, 0, 2, 6, 8):
+    for k in (0, 2, 6, 8):
         cb[k].wait_recv()
     fac2 = jnp.where(row == 0, 1.0, 2.0)
 
@@ -302,6 +335,8 @@
     c_yp.start()
     c_ym.start()
 
+    gather((1, 7), False)
+
     c_yp.wait_recv()
     c_ym.wait_recv()
     for g in range(3):
@@ -309,76 +344,14 @@
     c_xp.start()
     c_xm.start()
 
-    for k in (3, 5, 0, 2, 6, 8):
-        cd[k].wait_recv()
-
-    def pressure(i, _):
-        got = jnp.zeros((24, 128), F32)
-        for j in range(8):
-            nid = fl[i * 8 + j]
-            y = fx[i * 8 + j]
-            w8 = row8(hd[nid])
-            fun = stack3(jnp.concatenate([y[0:4], (y * w8)[0:4]], axis=0))
-            at = slice(j * 128, (j + 1) * 128)
-            got = got + dot(fun, qh[i, :, at], NT) + dot(fun, ql[i, :, at], NT)
-        p8 = sum3(got)
-        w_i = row8(hd[128 + i])
-        comb = w_i[0:4] * p8[0:4] + p8[4:8]
-        x = hf[128 + i] - 0.5
-        force = x * jnp.broadcast_to(comb[0:1], (4, 128)) - comb
-        for d in range(3):
-            pf[d, pl.ds(i, 1), :] = force[d + 1 : d + 2]
-        return 0
-
-    lax.fori_loop(0, 32, pressure, 0)
-    for d in range(3):
-        down = -1.0 if d == 2 else 0.0
-        o_fa[d] = jnp.where(f_on, PRESS_C * pf[d] + dr[d] + down, 0.0)
-
-    c_xp.wait_recv()
-    c_xm.wait_recv()
-    for d in range(3):
-        o_cp[d] = red[1, d] + (rx[0, d] + rx[1, d])
-
-    for group in (cf, cb, cd):
-        for k in group:
-            group[k].wait_send()
-    for c in (c_yp, c_ym, c_xp, c_xm):
-        c.wait_send()
-
-
-def contact_kernel(
-    bcnt, bpos, bvel, brad, bmass, cid, hist, hb, coupled, o_ba, o_h, ga, cnb, pu
-):
-    for b in range(16):
-        cnb[b : b + 1, :] = jnp.full((1, 128), bcnt[b], jnp.int32)
-
-    def block(b, _):
+    gather((0, 2, 6, 8), False)
+
+    def contact(b, _):
         st = pl.multiple_of(b * 128, 128)
-        ids8 = cid[:, pl.ds(st, 128)]
-        for q in range(8):
-            ids = row8(ids8[q : q + 1])
-            ln = ids & 127
-            bits = [(ids & (128 << k)) != 0 for k in range(4)]
-            tl = ids >> 11
-            out = None
-            for t in range(9):
-                vals = [
-                    jnp.take_along_axis(
-                        hb[t * 16 + r], ln, axis=1,
-                        mode="promise_in_bounds",
-                    )
-                    for r in range(16)
-                ]
-                for k in range(4):
-                    vals = [
-                        jnp.where(bits[k], vals[j + 1], vals[j]) for j in range(0, len(vals), 2)
-                    ]
-                out = vals[0] if out is None else jnp.where(tl == t, vals[0], out)
-            ga[q * 8 : q * 8 + 8, :] = out
-
-        ox, oy = tile_offsets(ids8 >> 11)
-        got = [ga[pl.ds(f, 8, stride=8), :] for f in range(8)]
+        ids = cid[:, pl.ds(st, 128)]
+        ox, oy = tile_offsets(ids >> 11)
+        base = b * 64
+        got = [ga[pl.ds(base + f, 8, stride=8), :] for f in range(8)]
         at = pl.ds(b, 1)
         r1 = row8(bpos[0, at, :]) - (got[1] + ox)
         r2 = row8(bpos[1, at, :]) - (got[2] + oy)
@@ -398,11 +371,46 @@
             o_h[d, :, pl.ds(st, 128)] = jnp.where(on, spring, 0.0)
         return 0
 
-    lax.fori_loop(0, 16, block, 0)
-    b_on = lax.broadcasted_iota(jnp.int32, (16, 128), 1) < cnb[...]
+    lax.fori_loop(0, 16, contact, 0)
+
+    for k in (3, 5, 0, 2, 6, 8):
+        cd[k].wait_recv()
+
+    def pressure(i, _):
+        got = jnp.zeros((24, 128), F32)
+        for j in range(8):
+            nid = fl[i * 8 + j]
+            y = fx[i * 8 + j]
+            w8 = row8(hd[nid])
+            fun = stack3(jnp.concatenate([y[0:4], (y * w8)[0:4]], axis=0))
+            at = slice(j * 128, (j + 1) * 128)
+            got = got + dot(fun, qh[i, :, at], NT) + dot(fun, ql[i, :, at], NT)
+        p8 = sum3(got)
+        w_i = row8(hd[128 + i])
+        comb = w_i[0:4] * p8[0:4] + p8[4:8]
+        x = hf[128 + i] - 0.5
+        force = x * jnp.broadcast_to(comb[0:1], (4, 128)) - comb
+        for d in range(3):
+            pf[d, pl.ds(i, 1), :] = force[d + 1 : d + 2]
+        return 0
+
+    lax.fori_loop(0, 32, pressure, 0)
     for d in range(3):
         down = -1.0 if d == 2 else 0.0
-        o_ba[d] = jnp.where(b_on, (pu[d] + coupled[d]) / bmass[...] + down, 0.0)
+        o_fa[d] = jnp.where(f_on, PRESS_C * pf[d] + dr[d] + down, 0.0)
+
+    c_xp.wait_recv()
+    c_xm.wait_recv()
+    for d in range(3):
+        down = -1.0 if d == 2 else 0.0
+        coupled = red[1, d] + (rx[0, d] + rx[1, d])
+        o_ba[d] = jnp.where(b_on, (pu[d] + coupled) / bmass[...] + down, 0.0)
+
+    for group in (cf, cb, cd):
+        for k in group:
+            group[k].wait_send()
+    for c in (c_yp, c_ym, c_xp, c_xm):
+        c.wait_send()
 
 
 def body(
@@ -413,24 +421,20 @@
     n_x, n_y = lax.axis_size("gx"), lax.axis_size("gy")
     vm = pl.BlockSpec(memory_space=pltpu.VMEM)
     sm = pl.BlockSpec(memory_space=pltpu.SMEM)
-    counts_b = boulder_counts.reshape(16)
-    pos_b = boulder_position.reshape(3, 16, 128)
-    vel_b = boulder_velocity.reshape(3, 16, 128)
-    rad_b = boulder_radius.reshape(16, 128)
-    mass_b = boulder_mass.reshape(16, 128)
-    fa, fd, hood, coupled = pl.pallas_call(
+    outs = pl.pallas_call(
         lambda *refs: kernel(*refs, n_x=n_x, n_y=n_y),
         name="step",
         out_shape=(
             jax.ShapeDtypeStruct((3, 32, 128), F32),
             jax.ShapeDtypeStruct((32, 128), F32),
-            jax.ShapeDtypeStruct((144, 8, 128), F32),
             jax.ShapeDtypeStruct((3, 16, 128), F32),
+            jax.ShapeDtypeStruct((3, 8, 2048), F32),
         ),
-        in_specs=[sm] * 4 + [vm] * 8,
+        in_specs=[sm] * 4 + [vm] * 10,
         out_specs=(vm,) * 4,
         scratch_shapes=[
             pltpu.VMEM((288, 4, 128), F32),
+            pltpu.VMEM((144, 8, 128), F32),
             pltpu.VMEM((288, 1, 128), F32),
             pltpu.VMEM((32, 128, 128), BF16),
             pltpu.VMEM((32, 128, 1024), BF16),
@@ -438,6 +442,7 @@
             pltpu.VMEM((256, 8, 128), F32),
             pltpu.VMEM((32, 8, 128), F32),
             pltpu.VMEM((32, 8, 128), F32),
+            pltpu.VMEM((1024, 128), F32),
             pltpu.VMEM((1024, 128), F32),
             pltpu.VMEM((3, 3, 3, 16, 128), F32),
             pltpu.VMEM((2, 3, 3, 16, 128), F32),
@@ -448,44 +453,30 @@
             pltpu.VMEM((32, 128), F32),
             pltpu.VMEM((3, 32, 128), F32),
             pltpu.VMEM((3, 32, 128), F32),
+            pltpu.VMEM((3, 16, 128), F32),
             pltpu.SemaphoreType.DMA((28,)),
             pltpu.SemaphoreType.DMA((28,)),
         ],
         compiler_params=pltpu.CompilerParams(
-            collective_id=0, has_side_effects=True, vmem_limit_bytes=48 * 1024 * 1024
+            collective_id=0, has_side_effects=True, vmem_limit_bytes=67043328
         ),
     )(
         fluid_lists.reshape(256),
         coupling_lists.reshape(128),
         fluid_counts.reshape(32),
-        counts_b,
+        boulder_counts.reshape(16),
         fluid_position.reshape(3, 32, 128),
         fluid_velocity.reshape(3, 32, 128),
         fluid_mass.reshape(32, 128),
         coupling_lists.reshape(1, 128),
-        pos_b,
-        vel_b,
-        rad_b,
-        mass_b,
+        boulder_position.reshape(3, 16, 128),
+        boulder_velocity.reshape(3, 16, 128),
+        boulder_radius.reshape(16, 128),
+        boulder_mass.reshape(16, 128),
+        contact_ids.reshape(8, 2048),
+        spring_history.reshape(3, 8, 2048),
     )
-    ba, ho = pl.pallas_call(
-        contact_kernel,
-        name="contact",
-        out_shape=(
-            jax.ShapeDtypeStruct((3, 16, 128), F32),
-            jax.ShapeDtypeStruct((3, 8, 2048), F32),
-        ),
-        in_specs=[sm] + [vm] * 8,
-        out_specs=(vm,) * 2,
-        scratch_shapes=[
-            pltpu.VMEM((64, 128), F32),
-            pltpu.VMEM((16, 128), jnp.int32),
-            pltpu.VMEM((3, 16, 128), F32),
-        ],
-    )(
-        counts_b, pos_b, vel_b, rad_b, mass_b,
-        contact_ids.reshape(8, 2048), spring_history.reshape(3, 8, 2048), hood, coupled,
-    )
+    fa, fd, ba, ho = outs
     return (
         fa.reshape(3, 1, 1, 4096),
         fd.reshape(1, 1, 4096),

time: 107 us -> 105 us (0.981)
  Pallas kernels: 97.6 us -> 95.9 us
    pallas_call x1 -> x0, Pallas kernels: 23.6 us -> none  [body(): pl.pallas_call(contact_kernel, name='contact', out_shape=(jax.ShapeDtypeS...]
    pallas_call x1, Pallas kernels: 74 us -> 95.9 us  [body(): pl.pallas_call(lambda *refs: kernel(*refs, n_x=n_x, n_y=n_y), name='step'...]
    unnamed x28 -> x14, local copies, waits for them, and re-layouts: 6.92 us -> 5.3 us
where the time goes in v1:
time: 105 us; the launch traced here: 104 us
  Pallas kernels  95.9 us (91%)
  local copies, waits for them, and re-layouts  7.19 us (7%)
    pallas_call x1, Pallas kernels, body(): pl.pallas_call(lambda *refs: kernel(*refs, n_x=n_x, n_y=n_y), name='step'...  95.9 us
    unnamed x14, local copies, waits for them, and re-layouts  5.3 us

profile of v1, /device:TPU:1, one launch (start us, length us, event | category | flops | bytes accessed | tf_op | source)
XLA Modules:
  0.0 103.8 jit_solution(2431926727290416813)
XLA Ops:
  0.6 0.0 copy-start.3
  0.6 0.7 copy-done.3
  1.3 0.1 copy.23
  1.4 0.6 reshape.69.refs_7_
  2.0 0.0 copy-start.2
  2.0 0.6 reshape.63.refs_1_
  2.6 0.1 copy-done.2
  2.7 0.1 copy.22
  2.8 0.7 reshape.62.refs_0_
  3.4 95.9 %step.1 = (f32[3,32,128]{2,1,0:T(8,128)}, f32[32,128]{1,0:T(8,128)}, f32[3,16,128]{2,1,0:T(8,128)}, f32[3,8,2048]{2,1,0:T(8,128)}) custom-call(s32[256]{0:T(256)} %reshape.62.refs_0_, s32[128]{0:T(128)} %reshape.63.refs_1_, s32[32]{0:T(128)} %bitcast.36, s32[16]{0:T(128)} %bitcast.37, f32[3,32,128]{2,1,0:T(8,128)} %bitcast.26, f32[3,32,128]{2,1,0:T(8,128)} %bitcast.27, ...), custom_call_target="tpu_custom_call" | custom-call | tf_op jit(solution)/shard_map/step/pallas_call | solution.py:424
  99.3 0.0 copy-start.1
  99.4 1.4 %copy.32 = f32[3,1,1,4096]{3,2,1,0:T(1,128)} copy(f32[3,1,1,4096]{3,2,1,0:T(1,128)} %bitcast.28) | data formatting | bytes 98304
  100.8 0.0 copy-done.1
  100.8 0.0 copy-start
  100.8 0.6 copy.33
  101.4 0.1 copy-done
  101.5 0.6 copy.34
  102.1 1.6 %copy.35 = f32[3,1,1,8,2048]{4,3,2,1,0:T(8,128)} copy(f32[3,1,1,8,2048]{4,3,2,1,0:T(8,128)} %bitcast.24) | data formatting | bytes 393216
Async XLA Ops:
  0.6 0.7 copy-start.3
  2.0 0.7 copy-start.2
  99.3 1.4 %copy-start.1 = (f32[32,128]{1,0:T(8,128)S(1)}, f32[32,128]{1,0:T(8,128)}, u32[]{:S(2)}) copy-start(f32[32,128]{1,0:T(8,128)} %get-tuple-element.9) | copy-start | bytes 49156
  100.8 0.7 copy-start

commit v2 on v1

--- a/solution.py
+++ b/solution.py
@@ -20,6 +20,10 @@
 DT = 0.05
 SOFT2 = 0.02**2
 PRESS_C = 6.0 / 0.3**2
+X_UNIT = 2.0**21
+V_HALF = 32766
+R_LOW = 0.03
+R_UNIT = ((1 << 17) - 4) / 0.04
 
 
 def rounded(x):
@@ -47,12 +51,13 @@
     return jnp.concatenate([h, m, h, m, l, h], axis=0).astype(BF16)
 
 
-def stack3(x):
-    return jnp.concatenate(split3(x), axis=0).astype(BF16)
-
-
-def sum3(x):
-    return x[0:8] + x[8:16] + x[16:24]
+def stack2(x):
+    hi = rounded(x)
+    return jnp.concatenate([hi, x - hi], axis=0).astype(BF16)
+
+
+def sum2(x):
+    return x[0:8] + x[8:16]
 
 
 def row8(x):
@@ -73,7 +78,7 @@
     fl, cl, fcnt, bcnt,
     fpos, fvel, fmass, clv, bpos, bvel, brad, bmass, cid, hist,
     o_fa, o_fd, o_ba, o_h,
-    hf, hb, hd, ut, qh, ql, fx, fu, fi, ga, sp, cp, ry, red, rx,
+    hf, hb, hd, ut, qh, ql, fx, fu, fi, hp, sc, ga, sp, cp, ry, red, rx,
     cnf, cnb, dens, dr, pf, pu, ssem, rsem,
     *, n_x, n_y,
 ):
@@ -141,12 +146,6 @@
     c_xp = copy(red.at[2], rx.at[0], 26, xp)
     c_xm = copy(red.at[0], rx.at[1], 27, xm)
 
-    pl.semaphore_wait(barrier, 4)
-    for k in (1, 7, 3, 5):
-        cf[k].start()
-    for k in (1, 7, 3, 5):
-        cb[k].start()
-
     u_planes = [fvel[d] for d in range(3)]
     mf_live = jnp.where(f_on, fmass[...], 0.0)
     one1 = jnp.ones((1, 128), F32)
@@ -173,21 +172,53 @@
 
     lax.fori_loop(0, 32, own_left, 0)
 
+    pl.semaphore_wait(barrier, 4)
+    for k in (1, 7, 3, 5):
+        cf[k].start()
+    for k in (1, 7, 3, 5):
+        cb[k].start()
+
+    def pack(t):
+        at = slice(t * 16, (t + 1) * 16)
+        plane = lambda f: hb[at, f, :]
+        vel = [plane(4 + d) for d in range(3)]
+        top = jnp.maximum(jnp.maximum(jnp.abs(vel[0]), jnp.abs(vel[1])), jnp.abs(vel[2]))
+        top = jnp.max(jnp.max(top, axis=0, keepdims=True), axis=1, keepdims=True)
+        top = jnp.maximum(jnp.broadcast_to(top, (8, 128)), 1e-30)
+        sc[t] = top * (1.0 / V_HALF)
+        inv = V_HALF / top[0:1]
+        coord = [
+            jnp.minimum((plane(1 + d) * X_UNIT).astype(jnp.int32), (1 << 21) - 1) for d in range(3)
+        ]
+        code = [(v * inv + (V_HALF + 1.5)).astype(jnp.int32) for v in vel]
+        rad = (jnp.maximum(plane(7) - R_LOW, 0.0) * R_UNIT + 1.5).astype(jnp.int32)
+        rad = jnp.where(plane(0) > 0.0, jnp.minimum(rad, (1 << 17) - 1), 0)
+        words = [(coord[d] << 11) | (code[d] >> 5) for d in range(3)]
+        words.append(
+            (rad << 15) | ((code[0] & 31) << 10) | ((code[1] & 31) << 5) | (code[2] & 31)
+        )
+        for w in range(4):
+            for half in range(2):
+                hp[pl.ds(t * 128 + half * 4 + w, 16, stride=8), :] = words[w]
+
     def gather(tiles, first):
+        for t in tiles:
+            pack(t)
+
         def block(b, _):
             st = pl.multiple_of(b * 128, 128)
             ids8 = cid[:, pl.ds(st, 128)]
-            for q in range(8):
-                ids = row8(ids8[q : q + 1])
+            for q in range(4):
+                ids = jnp.where(row < 4, row8(ids8[2 * q : 2 * q + 1]), row8(ids8[2 * q + 1 : 2 * q + 2]))
                 ln = ids & 127
                 bits = [(ids & (128 << k)) != 0 for k in range(4)]
                 tl = ids >> 11
-                at = pl.ds(pl.multiple_of(b * 64 + q * 8, 8), 8)
-                out = jnp.zeros((8, 128), F32) if first else ga[at, :]
+                at = pl.ds(pl.multiple_of(b * 32 + q * 8, 8), 8)
+                out = None if first else ga[at, :]
                 for t in tiles:
                     vals = [
                         jnp.take_along_axis(
-                            hb[t * 16 + r], ln, axis=1,
+                            hp[(t * 16 + r) * 8 : (t * 16 + r + 1) * 8, :], ln, axis=1,
                             mode="promise_in_bounds",
                         )
                         for r in range(16)
@@ -196,7 +227,7 @@
                         vals = [
                             jnp.where(bits[k], vals[j + 1], vals[j]) for j in range(0, len(vals), 2)
                         ]
-                    out = jnp.where(tl == t, vals[0], out)
+                    out = vals[0] if out is None else jnp.where(tl == t, vals[0], out)
                 ga[at, :] = out
             return 0
 
@@ -211,10 +242,6 @@
         cf[k].wait_recv()
     for k in (0, 2, 6, 8):
         cf[k].start()
-    for k in (1, 7):
-        cb[k].wait_recv()
-    for k in (0, 2, 6, 8):
-        cb[k].start()
     for k in (3, 5, 0, 2, 6, 8):
         cf[k].wait_recv()
 
@@ -259,7 +286,12 @@
         dens[pl.ds(i, 1), :] = total[0:1]
         return 0
 
-    lax.fori_loop(0, 32, density, 0)
+    lax.fori_loop(0, 16, density, 0)
+    for k in (1, 7):
+        cb[k].wait_recv()
+    for k in (0, 2, 6, 8):
+        cb[k].start()
+    lax.fori_loop(16, 32, density, 0)
     rho = fmass[...] + dens[...]
     weight = STIFF * (rho / REST - 1.0) / (rho * rho)
     for b in range(32):
@@ -290,31 +322,31 @@
             y = jnp.where(row == 0, c8, c8 * x)
             w = jnp.where(row < 4, y * (t8 * fac2), jnp.where(row == 4, c8 * (1.0 - t8 * n8), 0.0))
             cols.append(right_stack(w))
-            funs.append(stack3(jnp.where(row == 0, 1.0, raw)))
-        fside = stack3(fi[i])
-        pulled = jnp.zeros((24, 128), F32)
+            funs.append(stack2(jnp.where(row == 0, 1.0, raw)))
+        fside = stack2(fi[i])
+        pulled = jnp.zeros((16, 128), F32)
         for h in range(2):
             rhs = jnp.concatenate(cols[2 * h : 2 * h + 2], axis=1)
             u = jnp.maximum(dot(lhs, rhs, NN), 0.0)
             hi, lo = halves(u * u)
             fun = jnp.concatenate(funs[2 * h : 2 * h + 2], axis=1)
             pulled = pulled + dot(fun, hi, NT) + dot(fun, lo, NT)
-            back = sum3(dot(fside, hi, NN) + dot(fside, lo, NN))
+            back = sum2(dot(fside, hi, NN) + dot(fside, lo, NN))
             for g in range(2):
                 at = pl.ds(pl.multiple_of((i * 4 + 2 * h + g) * 8, 8), 8)
                 sp[at, :] = back[:, g * 128 : (g + 1) * 128]
-        d8 = sum3(pulled)
+        d8 = sum2(pulled)
         drag = d8 - fu[i] * row8(d8[0:1])
         for d in range(3):
             dr[d, pl.ds(i, 1), :] = drag[4 + d : 5 + d]
         return 0
 
-    lax.fori_loop(0, 32, coupling, 0)
-
+    lax.fori_loop(0, 20, coupling, 0)
     for k in (1, 7):
         cd[k].wait_recv()
     for k in (0, 2, 6, 8):
         cd[k].start()
+    lax.fori_loop(20, 32, coupling, 0)
 
     onehot = (
         lax.broadcasted_iota(jnp.int32, (144, 128), 0) == jnp.broadcast_to(clv[...], (144, 128))
@@ -335,8 +367,28 @@
     c_yp.start()
     c_ym.start()
 
-    gather((1, 7), False)
-
+    for k in (3, 5, 0, 2, 6, 8):
+        cd[k].wait_recv()
+
+    def pressure(i, _):
+        got = jnp.zeros((16, 128), F32)
+        for j in range(8):
+            nid = fl[i * 8 + j]
+            y = fx[i * 8 + j]
+            w8 = row8(hd[nid])
+            fun = stack2(jnp.concatenate([y[0:4], (y * w8)[0:4]], axis=0))
+            at = slice(j * 128, (j + 1) * 128)
+            got = got + dot(fun, qh[i, :, at], NT) + dot(fun, ql[i, :, at], NT)
+        p8 = sum2(got)
+        w_i = row8(hd[128 + i])
+        comb = w_i[0:4] * p8[0:4] + p8[4:8]
+        x = hf[128 + i] - 0.5
+        force = x * jnp.broadcast_to(comb[0:1], (4, 128)) - comb
+        for d in range(3):
+            pf[d, pl.ds(i, 1), :] = force[d + 1 : d + 2]
+        return 0
+
+    lax.fori_loop(0, 14, pressure, 0)
     c_yp.wait_recv()
     c_ym.wait_recv()
     for g in range(3):
@@ -344,23 +396,45 @@
     c_xp.start()
     c_xm.start()
 
+    lax.fori_loop(14, 32, pressure, 0)
+    for d in range(3):
+        down = -1.0 if d == 2 else 0.0
+        o_fa[d] = jnp.where(f_on, PRESS_C * pf[d] + dr[d] + down, 0.0)
+
+    gather((1, 7), False)
     gather((0, 2, 6, 8), False)
 
     def contact(b, _):
         st = pl.multiple_of(b * 128, 128)
         ids = cid[:, pl.ds(st, 128)]
-        ox, oy = tile_offsets(ids >> 11)
-        base = b * 64
-        got = [ga[pl.ds(base + f, 8, stride=8), :] for f in range(8)]
+        tile = ids >> 11
+        ox, oy = tile_offsets(tile)
+        base = b * 32
+        words = [ga[pl.ds(base + w, 8, stride=4), :] for w in range(4)]
+        step = sc[0]
+        for t in range(1, 9):
+            step = jnp.where(tile == t, sc[t], step)
+        low = words[3]
+        xyz = [
+            ((words[d] >> 11) & ((1 << 21) - 1)).astype(F32) * (1.0 / X_UNIT) + 0.5 / X_UNIT
+            for d in range(3)
+        ]
+        pvel = [
+            ((((words[d] & 2047) << 5) | ((low >> (10 - 5 * d)) & 31)) - (V_HALF + 1)).astype(F32)
+            * step
+            for d in range(3)
+        ]
+        code = (low >> 15) & ((1 << 17) - 1)
+        prad = (code - 1).astype(F32) * (1.0 / R_UNIT) + R_LOW
         at = pl.ds(b, 1)
-        r1 = row8(bpos[0, at, :]) - (got[1] + ox)
-        r2 = row8(bpos[1, at, :]) - (got[2] + oy)
-        r3 = row8(bpos[2, at, :]) - got[3]
+        r1 = row8(bpos[0, at, :]) - (xyz[0] + ox)
+        r2 = row8(bpos[1, at, :]) - (xyz[1] + oy)
+        r3 = row8(bpos[2, at, :]) - xyz[2]
         dist = jnp.sqrt((r1 * r1 + r2 * r2) + r3 * r3 + SOFT2)
         inv = 1.0 / dist
         nrm = (r1 * inv, r2 * inv, r3 * inv)
-        inter = jnp.where(got[0] > 0.0, jnp.maximum(row8(brad[at, :]) + got[7] - dist, 0.0), 0.0)
-        rel = [row8(bvel[d, at, :]) - got[4 + d] for d in range(3)]
+        inter = jnp.where(code > 0, jnp.maximum(row8(brad[at, :]) + prad - dist, 0.0), 0.0)
+        rel = [row8(bvel[d, at, :]) - pvel[d] for d in range(3)]
         along = (rel[0] * nrm[0] + rel[1] * nrm[1]) + rel[2] * nrm[2]
         touch = jnp.minimum(inter * 100.0, 1.0)
         on = lax.broadcasted_iota(jnp.int32, (8, 128), 1) < jnp.broadcast_to(cnb[at, :], (8, 128))
@@ -372,32 +446,6 @@
         return 0
 
     lax.fori_loop(0, 16, contact, 0)
-
-    for k in (3, 5, 0, 2, 6, 8):
-        cd[k].wait_recv()
-
-    def pressure(i, _):
-        got = jnp.zeros((24, 128), F32)
-        for j in range(8):
-            nid = fl[i * 8 + j]
-            y = fx[i * 8 + j]
-            w8 = row8(hd[nid])
-            fun = stack3(jnp.concatenate([y[0:4], (y * w8)[0:4]], axis=0))
-            at = slice(j * 128, (j + 1) * 128)
-            got = got + dot(fun, qh[i, :, at], NT) + dot(fun, ql[i, :, at], NT)
-        p8 = sum3(got)
-        w_i = row8(hd[128 + i])
-        comb = w_i[0:4] * p8[0:4] + p8[4:8]
-        x = hf[128 + i] - 0.5
-        force = x * jnp.broadcast_to(comb[0:1], (4, 128)) - comb
-        for d in range(3):
-            pf[d, pl.ds(i, 1), :] = force[d + 1 : d + 2]
-        return 0
-
-    lax.fori_loop(0, 32, pressure, 0)
-    for d in range(3):
-        down = -1.0 if d == 2 else 0.0
-        o_fa[d] = jnp.where(f_on, PRESS_C * pf[d] + dr[d] + down, 0.0)
 
     c_xp.wait_recv()
     c_xm.wait_recv()
@@ -442,7 +490,9 @@
             pltpu.VMEM((256, 8, 128), F32),
             pltpu.VMEM((32, 8, 128), F32),
             pltpu.VMEM((32, 8, 128), F32),
-            pltpu.VMEM((1024, 128), F32),
+            pltpu.VMEM((1152, 128), jnp.int32),
+            pltpu.VMEM((9, 8, 128), F32),
+            pltpu.VMEM((512, 128), jnp.int32),
             pltpu.VMEM((1024, 128), F32),
             pltpu.VMEM((3, 3, 3, 16, 128), F32),
             pltpu.VMEM((2, 3, 3, 16, 128), F32),

time: 105 us -> 95.8 us (0.912)
  Pallas kernels: 95.9 us -> 87.6 us
    pallas_call x1, Pallas kernels: 95.9 us -> 87.6 us  [body(): pl.pallas_call(lambda *refs: kernel(*refs, n_x=n_x, n_y=n_y), name='step'...]
where the time goes in v2:
time: 95.8 us; the launch traced here: 95.4 us
  Pallas kernels  87.6 us (91%)
  local copies, waits for them, and re-layouts  7.19 us (8%)
    pallas_call x1, Pallas kernels, body(): pl.pallas_call(lambda *refs: kernel(*refs, n_x=n_x, n_y=n_y), name='step'...  87.6 us
    unnamed x14, local copies, waits for them, and re-layouts  5.3 us

profile of v2, /device:TPU:1, one launch (start us, length us, event | category | flops | bytes accessed | tf_op | source)
XLA Modules:
  0.0 95.4 jit_solution(8969861905570481619)
XLA Ops:
  0.6 0.0 copy-start.3
  0.6 0.7 copy-done.3
  1.3 0.1 copy.23
  1.4 0.6 reshape.69.refs_7_
  2.0 0.0 copy-start.2
  2.0 0.6 reshape.63.refs_1_
  2.6 0.1 copy-done.2
  2.7 0.1 copy.22
  2.8 0.7 reshape.62.refs_0_
  3.4 87.6 %step.1 = (f32[3,32,128]{2,1,0:T(8,128)}, f32[32,128]{1,0:T(8,128)}, f32[3,16,128]{2,1,0:T(8,128)}, f32[3,8,2048]{2,1,0:T(8,128)}) custom-call(s32[256]{0:T(256)} %reshape.62.refs_0_, s32[128]{0:T(128)} %reshape.63.refs_1_, s32[32]{0:T(128)} %bitcast.36, s32[16]{0:T(128)} %bitcast.37, f32[3,32,128]{2,1,0:T(8,128)} %bitcast.26, f32[3,32,128]{2,1,0:T(8,128)} %bitcast.27, ...), custom_call_target="tpu_custom_call" | custom-call | tf_op jit(solution)/shard_map/step/pallas_call | solution.py:472
  91.0 0.0 copy-start.1
  91.0 1.4 %copy.32 = f32[3,1,1,4096]{3,2,1,0:T(1,128)} copy(f32[3,1,1,4096]{3,2,1,0:T(1,128)} %bitcast.28) | data formatting | bytes 98304
  92.5 0.0 copy-done.1
  92.5 0.0 copy-start
  92.5 0.6 copy.33
  93.1 0.1 copy-done
  93.2 0.6 copy.34
  93.8 1.6 %copy.35 = f32[3,1,1,8,2048]{4,3,2,1,0:T(8,128)} copy(f32[3,1,1,8,2048]{4,3,2,1,0:T(8,128)} %bitcast.24) | data formatting | bytes 393216
Async XLA Ops:
  0.6 0.7 copy-start.3
  2.0 0.7 copy-start.2
  91.0 1.4 %copy-start.1 = (f32[32,128]{1,0:T(8,128)S(1)}, f32[32,128]{1,0:T(8,128)}, u32[]{:S(2)}) copy-start(f32[32,128]{1,0:T(8,128)} %get-tuple-element.9) | copy-start | bytes 49156
  92.5 0.7 copy-start

commit v3 on v2

--- a/solution.py
+++ b/solution.py
@@ -26,6 +26,15 @@
 R_UNIT = ((1 << 17) - 4) / 0.04
 
 
+def paired(lo, hi, one):
+    def two(i, _):
+        for k in range(4):
+            one(4 * i + k, 0)
+        return 0
+
+    lax.fori_loop(lo // 4, hi // 4, two, 0)
+
+
 def rounded(x):
     return x.astype(BF16).astype(F32)
 
@@ -41,25 +50,6 @@
     return lax.dot_general(a, b, dims, preferred_element_type=F32)
 
 
-def left_stack(x):
-    h, m, l = split3(x)
-    return jnp.concatenate([h, h, m, m, h, l], axis=0)
-
-
-def right_stack(x):
-    h, m, l = split3(x)
-    return jnp.concatenate([h, m, h, m, l, h], axis=0).astype(BF16)
-
-
-def stack2(x):
-    hi = rounded(x)
-    return jnp.concatenate([hi, x - hi], axis=0).astype(BF16)
-
-
-def sum2(x):
-    return x[0:8] + x[8:16]
-
-
 def row8(x):
     return jnp.broadcast_to(x, (8, x.shape[-1]))
 
@@ -78,7 +68,7 @@
     fl, cl, fcnt, bcnt,
     fpos, fvel, fmass, clv, bpos, bvel, brad, bmass, cid, hist,
     o_fa, o_fd, o_ba, o_h,
-    hf, hb, hd, ut, qh, ql, fx, fu, fi, hp, sc, ga, sp, cp, ry, red, rx,
+    hf, hb, hd, ut, qh, ql, stg, tf, tb, gb, ft, fi, hp, sc, ga, sp, cp, ry, red, rx,
     cnf, cnb, dens, dr, pf, pu, ssem, rsem,
     *, n_x, n_y,
 ):
@@ -102,22 +92,13 @@
         cnb[b : b + 1, :] = jnp.full((1, 128), bcnt[b], jnp.int32)
     f_on = lane < cnf[...]
     b_on = lane[:16] < cnb[...]
-    croot = jnp.where(f_on, jnp.exp(jnp.log(fmass[...]) * (1.0 / 3.0)), 0.0)
-    for b in range(32):
-        s = slice(b, b + 1)
-        hf[128 + b] = jnp.concatenate(
-            [croot[s], fpos[0, s, :], fpos[1, s, :], fpos[2, s, :]], axis=0
-        )
-    bm_live = jnp.where(b_on, bmass[...], 0.0)
-    for b in range(16):
-        s = slice(b, b + 1)
-        hb[64 + b] = jnp.concatenate(
-            [bm_live[s]]
-            + [bpos[d, s, :] for d in range(3)]
-            + [bvel[d, s, :] for d in range(3)]
-            + [brad[s, :]],
-            axis=0,
-        )
+    hf[4, 0] = jnp.where(f_on, jnp.exp(jnp.log(fmass[...]) * (1.0 / 3.0)), 0.0)
+    hb[4, 0] = jnp.where(b_on, bmass[...], 0.0)
+    for d in range(3):
+        hf[4, 1 + d] = fpos[d]
+        hb[4, 1 + d] = bpos[d]
+        hb[4, 4 + d] = bvel[d]
+    hb[4, 7] = brad[...]
 
     def copy(src, dst, k, dev):
         return pltpu.make_async_remote_copy(
@@ -125,8 +106,8 @@
             device_id=dev, device_id_type=MESH,
         )
 
-    def halo(ref, width, base):
-        at = lambda t: ref.at[pl.ds(t * width, width)]
+    def halo(ref, base):
+        at = lambda t: ref.at[t]
         return {
             1: copy(at(4), at(1), base + 0, xp),
             7: copy(at(4), at(7), base + 1, xm),
@@ -138,39 +119,35 @@
             8: copy(at(7), at(8), base + 7, ym),
         }
 
-    cf = halo(hf, 32, 0)
-    cb = halo(hb, 16, 8)
-    cd = halo(hd, 32, 16)
+    cf = halo(hf, 0)
+    cb = halo(hb, 8)
+    cd = halo(hd, 16)
     c_yp = copy(cp.at[2], ry.at[0], 24, yp)
     c_ym = copy(cp.at[0], ry.at[1], 25, ym)
     c_xp = copy(red.at[2], rx.at[0], 26, xp)
     c_xm = copy(red.at[0], rx.at[1], 27, xm)
 
-    u_planes = [fvel[d] for d in range(3)]
-    mf_live = jnp.where(f_on, fmass[...], 0.0)
     one1 = jnp.ones((1, 128), F32)
-    zero3 = jnp.zeros((3, 128), F32)
-    for b in range(32):
-        s = slice(b, b + 1)
-        v = jnp.concatenate(
-            [one1, zero3, u_planes[0][s], u_planes[1][s], u_planes[2][s], zero3[:1]], axis=0
+    zeros = lambda n: jnp.zeros((n, 128), F32)
+
+    def own_left(i, _):
+        at = pl.ds(i, 1)
+        x = [fpos[d, at, :] - 0.5 for d in range(3)]
+        norm = -(x[0] * x[0] + x[1] * x[1] + x[2] * x[2])
+        h, m, l = split3(jnp.concatenate([norm, x[0], x[1], x[2], one1, zeros(3)], axis=0))
+        h, m, l = h[0:5], m[0:5], l[0:5]
+        full = jnp.concatenate(
+            [h, h, h, zeros(1), m, m, zeros(6), l, zeros(91)], axis=0
         )
-        fu[b] = v
-        fi[b] = v * row8(mf_live[s])
-
-    zeros80 = jnp.zeros((80, 128), F32)
-
-    def own_left(i, _):
-        raw = hf[128 + i]
-        x = raw - 0.5
-        x1, x2, x3 = x[1:2], x[2:3], x[3:4]
-        norm = -(x1 * x1 + x2 * x2 + x3 * x3)
-        u8 = jnp.concatenate([norm, x1, x2, x3, one1, zero3], axis=0)
-        full = jnp.concatenate([left_stack(u8), zeros80], axis=0)
         ut[i] = full.T.astype(BF16)
         return 0
 
-    lax.fori_loop(0, 32, own_left, 0)
+    paired(0, 32, own_left)
+    mf_live = jnp.where(f_on, fmass[...], 0.0)
+    for r, v in enumerate([mf_live] + [mf_live * fvel[d] for d in range(3)]):
+        hi = rounded(v)
+        fi[pl.ds(r, 32, stride=8), :] = hi
+        fi[pl.ds(4 + r, 32, stride=8), :] = v - hi
 
     pl.semaphore_wait(barrier, 4)
     for k in (1, 7, 3, 5):
@@ -178,9 +155,48 @@
     for k in (1, 7, 3, 5):
         cb[k].start()
 
+    def settle(dst, t, blocks):
+        def four(g, _):
+            for j in range(4):
+                at = t * blocks + g * 4 + j
+                dst[at] = stg[pl.ds(pl.multiple_of(at * 16, 16), 16), :].astype(BF16)
+            return 0
+
+        lax.fori_loop(0, blocks // 4, four, 0)
+
+    def centred(ref, t):
+        return [ref[t, 1] + (t // 3 - 1.5), ref[t, 2] + (t % 3 - 1.5), ref[t, 3] - 0.5]
+
+    def pair_rows(t, blocks, c, x, scale):
+        n = (x[0] * x[0] + x[1] * x[1]) + x[2] * x[2]
+        cs = c * scale
+        rows = [cs] + [(2.0 * cs) * v for v in x] + [c * (1.0 - scale * n)]
+        for r, v in enumerate(rows):
+            for k, part in enumerate(split3(v)):
+                stg[pl.ds(t * blocks * 16 + 5 * k + r, blocks, stride=16), :] = part
+        stg[pl.ds(t * blocks * 16 + 15, blocks, stride=16), :] = zeros(blocks)
+
+    def fluid_table(t):
+        pair_rows(t, 32, hf[t, 0], centred(hf, t), INV_H2)
+        settle(tf, t, 32)
+
+    def boulder_table(t):
+        m = hb[t, 0]
+        c = jnp.where(m > 0.0, jnp.sqrt(jnp.maximum(m, 1e-30)), 0.0)
+        reach = hb[t, 7] + COUPLE
+        pair_rows(t, 16, c, centred(hb, t), 1.0 / (reach * reach))
+        settle(tb, t, 16)
+        ones = jnp.ones((16, 128), F32)
+        for r in range(4):
+            v = ones if r == 0 else hb[t, 3 + r]
+            hi = rounded(v)
+            base = t * 256 + r
+            stg[pl.ds(base, 16, stride=16), :] = hi
+            stg[pl.ds(base + 4, 16, stride=16), :] = v - hi
+        settle(gb, t, 16)
+
     def pack(t):
-        at = slice(t * 16, (t + 1) * 16)
-        plane = lambda f: hb[at, f, :]
+        plane = lambda f: hb[t, f]
         vel = [plane(4 + d) for d in range(3)]
         top = jnp.maximum(jnp.maximum(jnp.abs(vel[0]), jnp.abs(vel[1])), jnp.abs(vel[2]))
         top = jnp.max(jnp.max(top, axis=0, keepdims=True), axis=1, keepdims=True)
@@ -233,50 +249,42 @@
 
         lax.fori_loop(0, 16, block, 0)
 
+    fluid_table(4)
+    boulder_table(4)
+    cf[3].wait_recv()
+    cf[5].wait_recv()
+    fluid_table(3)
+    fluid_table(5)
     gather((4,), True)
-    cb[3].wait_recv()
-    cb[5].wait_recv()
-    gather((3, 5), False)
 
     for k in (1, 7):
         cf[k].wait_recv()
     for k in (0, 2, 6, 8):
         cf[k].start()
-    for k in (3, 5, 0, 2, 6, 8):
+    fluid_table(1)
+    fluid_table(7)
+    cb[3].wait_recv()
+    cb[5].wait_recv()
+    boulder_table(3)
+    boulder_table(5)
+    for k in (0, 2, 6, 8):
         cf[k].wait_recv()
-
-    coord = (row >= 1) & (row <= 3)
-    fac = jnp.where(row == 0, INV_H2, 2.0 * INV_H2)
+        fluid_table(k)
+
     ones8 = jnp.ones((8, 128), BF16)
-    zeros4 = jnp.zeros((4, 128), F32)
 
     def density(i, _):
         lhs = ut[i][:, 0:48]
         acc = jnp.zeros((128, 128), F32)
         for jj in range(4):
-            cols = []
-            for h in range(2):
-                j = jj * 2 + h
-                nid = fl[i * 8 + j]
-                ox, oy = tile_offsets(nid >> 5)
-                raw = jnp.concatenate([hf[nid], zeros4], axis=0)
-                shift = jnp.where(
-                    row == 1, ox - 0.5, jnp.where(row == 2, oy - 0.5, -0.5)
-                )
-                x = jnp.where(coord, raw + shift, 0.0)
-                c8 = row8(raw[0:1])
-                n8 = jnp.sum(x * x, axis=0, keepdims=True)
-                y = jnp.where(row == 0, c8, c8 * x)
-                fx[i * 8 + j] = y
-                w = jnp.where(row < 4, y * fac, jnp.where(row == 4, c8 * (1.0 - INV_H2 * n8), 0.0))
-                cols.append(right_stack(w))
-            u = jnp.maximum(dot(lhs, jnp.concatenate(cols, axis=1), NN), 0.0)
+            t2 = jnp.concatenate([tf[fl[i * 8 + jj * 2]], tf[fl[i * 8 + jj * 2 + 1]]], axis=1)
+            u = jnp.maximum(dot(lhs, jnp.concatenate([t2, t2, t2], axis=0), NN), 0.0)
             sq = u * u
             cube = sq * u
             acc = acc + (cube[:, 0:128] + cube[:, 128:256])
-            hi, lo = halves(sq)
-            qh[i, :, jj * 256 : (jj + 1) * 256] = hi
-            ql[i, :, jj * 256 : (jj + 1) * 256] = lo
+            at = slice(jj * 256, (jj + 1) * 256)
+            qh[i, :, at] = sq.astype(BF16)
+            ql[i, :, at] = (sq - qh[i, :, at].astype(F32)).astype(BF16)
         a, b, c = split3(acc)
         total = (
             dot(ones8, a.astype(BF16), NT)
@@ -286,122 +294,113 @@
         dens[pl.ds(i, 1), :] = total[0:1]
         return 0
 
-    lax.fori_loop(0, 16, density, 0)
+    paired(0, 16, density)
     for k in (1, 7):
         cb[k].wait_recv()
     for k in (0, 2, 6, 8):
         cb[k].start()
-    lax.fori_loop(16, 32, density, 0)
+    paired(16, 32, density)
     rho = fmass[...] + dens[...]
-    weight = STIFF * (rho / REST - 1.0) / (rho * rho)
-    for b in range(32):
-        hd[128 + b] = weight[b : b + 1]
+    hd[4] = STIFF * (rho / REST - 1.0) / (rho * rho)
     for k in (1, 7, 3, 5):
         cd[k].start()
     o_fd[...] = jnp.where(f_on, rho, 0.0)
 
+    boulder_table(1)
+    boulder_table(7)
     for k in (0, 2, 6, 8):
         cb[k].wait_recv()
-    fac2 = jnp.where(row == 0, 1.0, 2.0)
+        boulder_table(k)
 
     def coupling(i, _):
         lhs = ut[i][:, 0:48]
-        cols = []
-        funs = []
-        for j in range(4):
-            nid = cl[i * 4 + j]
-            ox, oy = tile_offsets(nid >> 4)
-            raw = hb[nid]
-            shift = jnp.where(row == 1, ox - 0.5, jnp.where(row == 2, oy - 0.5, -0.5))
-            x = jnp.where(coord, raw + shift, 0.0)
-            m8 = row8(raw[0:1])
-            c8 = jnp.where(m8 > 0.0, jnp.sqrt(jnp.maximum(m8, 1e-30)), 0.0)
-            reach = row8(raw[7:8]) + COUPLE
-            t8 = 1.0 / (reach * reach)
-            n8 = jnp.sum(x * x, axis=0, keepdims=True)
-            y = jnp.where(row == 0, c8, c8 * x)
-            w = jnp.where(row < 4, y * (t8 * fac2), jnp.where(row == 4, c8 * (1.0 - t8 * n8), 0.0))
-            cols.append(right_stack(w))
-            funs.append(stack2(jnp.where(row == 0, 1.0, raw)))
-        fside = stack2(fi[i])
+        fside = fi[pl.ds(pl.multiple_of(i * 8, 8), 8), :].astype(BF16)
         pulled = jnp.zeros((16, 128), F32)
         for h in range(2):
-            rhs = jnp.concatenate(cols[2 * h : 2 * h + 2], axis=1)
-            u = jnp.maximum(dot(lhs, rhs, NN), 0.0)
+            n0, n1 = cl[i * 4 + 2 * h], cl[i * 4 + 2 * h + 1]
+            t2 = jnp.concatenate([tb[n0], tb[n1]], axis=1)
+            u = jnp.maximum(dot(lhs, jnp.concatenate([t2, t2, t2], axis=0), NN), 0.0)
             hi, lo = halves(u * u)
-            fun = jnp.concatenate(funs[2 * h : 2 * h + 2], axis=1)
+            fun = jnp.concatenate([gb[n0], gb[n1]], axis=1)
             pulled = pulled + dot(fun, hi, NT) + dot(fun, lo, NT)
-            back = sum2(dot(fside, hi, NN) + dot(fside, lo, NN))
+            back = dot(fside, hi, NN) + dot(fside, lo, NN)
             for g in range(2):
                 at = pl.ds(pl.multiple_of((i * 4 + 2 * h + g) * 8, 8), 8)
                 sp[at, :] = back[:, g * 128 : (g + 1) * 128]
-        d8 = sum2(pulled)
-        drag = d8 - fu[i] * row8(d8[0:1])
-        for d in range(3):
-            dr[d, pl.ds(i, 1), :] = drag[4 + d : 5 + d]
+        d4 = pulled[0:4] + pulled[4:8]
+        for r in range(4):
+            dr[r, pl.ds(i, 1), :] = d4[r : r + 1]
         return 0
 
-    lax.fori_loop(0, 20, coupling, 0)
+    paired(0, 20, coupling)
     for k in (1, 7):
         cd[k].wait_recv()
     for k in (0, 2, 6, 8):
         cd[k].start()
-    lax.fori_loop(20, 32, coupling, 0)
+    paired(20, 32, coupling)
 
     onehot = (
         lax.broadcasted_iota(jnp.int32, (144, 128), 0) == jnp.broadcast_to(clv[...], (144, 128))
     ).astype(F32).astype(BF16)
 
     def reduced(r):
-        parts = split3(sp[pl.ds(r, 128, stride=8), :])
-        m = jnp.concatenate([v.astype(BF16) for v in parts], axis=1)
+        both = sp[pl.ds(r, 128, stride=8), :] + sp[pl.ds(r + 4, 128, stride=8), :]
+        m = jnp.concatenate([v.astype(BF16) for v in split3(both)], axis=1)
         got = dot(onehot, m, NN)
         return got[:, 0:128] + got[:, 128:256] + got[:, 256:384]
 
     mass_sum = reduced(0)
     for d in range(3):
-        vel = hb[:, 4 + d, :]
-        part = reduced(4 + d) - vel * mass_sum
+        pulls = reduced(1 + d)
         for t in range(9):
-            cp[t % 3, t // 3, d] = part[t * 16 : (t + 1) * 16]
+            at = slice(t * 16, (t + 1) * 16)
+            cp[t % 3, t // 3, d] = pulls[at] - hb[t, 4 + d] * mass_sum[at]
     c_yp.start()
     c_ym.start()
 
+    def press_table(t):
+        c = hf[t, 0]
+        rows = [c] + [c * v for v in centred(hf, t)]
+        w = hd[t]
+        rows = rows + [w * v for v in rows]
+        for r, v in enumerate(rows):
+            hi = rounded(v)
+            base = t * 512 + r
+            stg[pl.ds(base, 32, stride=16), :] = hi
+            stg[pl.ds(base + 8, 32, stride=16), :] = v - hi
+        settle(ft, t, 32)
+
+    for k in (4, 1, 7):
+        press_table(k)
     for k in (3, 5, 0, 2, 6, 8):
         cd[k].wait_recv()
+        press_table(k)
 
     def pressure(i, _):
-        got = jnp.zeros((16, 128), F32)
-        for j in range(8):
-            nid = fl[i * 8 + j]
-            y = fx[i * 8 + j]
-            w8 = row8(hd[nid])
-            fun = stack2(jnp.concatenate([y[0:4], (y * w8)[0:4]], axis=0))
-            at = slice(j * 128, (j + 1) * 128)
-            got = got + dot(fun, qh[i, :, at], NT) + dot(fun, ql[i, :, at], NT)
-        p8 = sum2(got)
-        w_i = row8(hd[128 + i])
-        comb = w_i[0:4] * p8[0:4] + p8[4:8]
-        x = hf[128 + i] - 0.5
-        force = x * jnp.broadcast_to(comb[0:1], (4, 128)) - comb
+        fun = jnp.concatenate([ft[fl[i * 8 + j]] for j in range(8)], axis=1)
+        got = dot(fun, qh[i], NT) + dot(fun, ql[i], NT)
+        p8 = got[0:8] + got[8:16]
+        at = pl.ds(i, 1)
+        w_i = hd[4, at, :]
+        comb = [w_i * p8[r : r + 1] + p8[4 + r : 5 + r] for r in range(4)]
         for d in range(3):
-            pf[d, pl.ds(i, 1), :] = force[d + 1 : d + 2]
+            pf[d, at, :] = (fpos[d, at, :] - 0.5) * comb[0] - comb[d + 1]
         return 0
 
-    lax.fori_loop(0, 14, pressure, 0)
+    paired(0, 16, pressure)
     c_yp.wait_recv()
     c_ym.wait_recv()
     for g in range(3):
         red[g] = cp[1, g] + (ry[0, g] + ry[1, g])
     c_xp.start()
     c_xm.start()
-
-    lax.fori_loop(14, 32, pressure, 0)
+    paired(16, 32, pressure)
     for d in range(3):
         down = -1.0 if d == 2 else 0.0
-        o_fa[d] = jnp.where(f_on, PRESS_C * pf[d] + dr[d] + down, 0.0)
-
-    gather((1, 7), False)
+        drag = dr[1 + d] - fvel[d] * dr[0]
+        o_fa[d] = jnp.where(f_on, PRESS_C * pf[d] + drag + down, 0.0)
+
+    gather((3, 5, 1, 7), False)
     gather((0, 2, 6, 8), False)
 
     def contact(b, _):
@@ -481,15 +480,18 @@
         in_specs=[sm] * 4 + [vm] * 10,
         out_specs=(vm,) * 4,
         scratch_shapes=[
-            pltpu.VMEM((288, 4, 128), F32),
-            pltpu.VMEM((144, 8, 128), F32),
-            pltpu.VMEM((288, 1, 128), F32),
+            pltpu.VMEM((9, 4, 32, 128), F32),
+            pltpu.VMEM((9, 8, 16, 128), F32),
+            pltpu.VMEM((9, 32, 128), F32),
             pltpu.VMEM((32, 128, 128), BF16),
             pltpu.VMEM((32, 128, 1024), BF16),
             pltpu.VMEM((32, 128, 1024), BF16),
-            pltpu.VMEM((256, 8, 128), F32),
-            pltpu.VMEM((32, 8, 128), F32),
-            pltpu.VMEM((32, 8, 128), F32),
+            pltpu.VMEM((4608, 128), F32),
+            pltpu.VMEM((288, 16, 128), BF16),
+            pltpu.VMEM((144, 16, 128), BF16),
+            pltpu.VMEM((144, 16, 128), BF16),
+            pltpu.VMEM((288, 16, 128), BF16),
+            pltpu.VMEM((256, 128), F32),
             pltpu.VMEM((1152, 128), jnp.int32),
             pltpu.VMEM((9, 8, 128), F32),
             pltpu.VMEM((512, 128), jnp.int32),
@@ -501,7 +503,7 @@
             pltpu.VMEM((32, 128), jnp.int32),
             pltpu.VMEM((16, 128), jnp.int32),
             pltpu.VMEM((32, 128), F32),
-            pltpu.VMEM((3, 32, 128), F32),
+            pltpu.VMEM((4, 32, 128), F32),
             pltpu.VMEM((3, 32, 128), F32),
             pltpu.VMEM((3, 16, 128), F32),
             pltpu.SemaphoreType.DMA((28,)),

time: 95.8 us -> 80 us (0.84)
  Pallas kernels: 87.6 us -> 71.8 us
    pallas_call x1, Pallas kernels: 87.6 us -> 71.8 us  [body(): pl.pallas_call(lambda *refs: kernel(*refs, n_x=n_x, n_y=n_y), name='step'...]
where the time goes in v3:
time: 80 us; the launch traced here: 79.7 us
  Pallas kernels  71.8 us (90%)
  local copies, waits for them, and re-layouts  7.19 us (9%)
    pallas_call x1, Pallas kernels, body(): pl.pallas_call(lambda *refs: kernel(*refs, n_x=n_x, n_y=n_y), name='step'...  71.8 us
    unnamed x14, local copies, waits for them, and re-layouts  5.3 us

profile of v3, /device:TPU:1, one launch (start us, length us, event | category | flops | bytes accessed | tf_op | source)
XLA Modules:
  0.0 79.7 jit_solution(10197208926649623860)
XLA Ops:
  0.6 0.0 copy-start.3
  0.6 0.7 copy-done.3
  1.3 0.1 copy.23
  1.4 0.6 reshape.69.refs_7_
  2.0 0.0 copy-start.2
  2.0 0.6 reshape.63.refs_1_
  2.6 0.1 copy-done.2
  2.7 0.1 copy.22
  2.8 0.7 reshape.62.refs_0_
  3.4 71.8 %step.1 = (f32[3,32,128]{2,1,0:T(8,128)}, f32[32,128]{1,0:T(8,128)}, f32[3,16,128]{2,1,0:T(8,128)}, f32[3,8,2048]{2,1,0:T(8,128)}) custom-call(s32[256]{0:T(256)} %reshape.62.refs_0_, s32[128]{0:T(128)} %reshape.63.refs_1_, s32[32]{0:T(128)} %bitcast.36, s32[16]{0:T(128)} %bitcast.37, f32[3,32,128]{2,1,0:T(8,128)} %bitcast.26, f32[3,32,128]{2,1,0:T(8,128)} %bitcast.27, ...), custom_call_target="tpu_custom_call" | custom-call | tf_op jit(solution)/shard_map/step/pallas_call | solution.py:471
  75.3 0.0 copy-start.1
  75.3 1.4 %copy.32 = f32[3,1,1,4096]{3,2,1,0:T(1,128)} copy(f32[3,1,1,4096]{3,2,1,0:T(1,128)} %bitcast.28) | data formatting | bytes 98304
  76.7 0.0 copy-done.1
  76.7 0.0 copy-start
  76.7 0.6 copy.33
  77.3 0.1 copy-done
  77.5 0.6 copy.34
  78.1 1.6 %copy.35 = f32[3,1,1,8,2048]{4,3,2,1,0:T(8,128)} copy(f32[3,1,1,8,2048]{4,3,2,1,0:T(8,128)} %bitcast.24) | data formatting | bytes 393216
Async XLA Ops:
  0.6 0.7 copy-start.3
  2.0 0.7 copy-start.2
  75.3 1.4 %copy-start.1 = (f32[32,128]{1,0:T(8,128)S(1)}, f32[32,128]{1,0:T(8,128)}, u32[]{:S(2)}) copy-start(f32[32,128]{1,0:T(8,128)} %get-tuple-element.9) | copy-start | bytes 49156
  76.7 0.7 copy-start

commit v4 on v3

--- a/solution.py
+++ b/solution.py
@@ -35,6 +35,17 @@
     lax.fori_loop(lo // 4, hi // 4, two, 0)
 
 
+def beside(lo, hi, one, extra):
+    def step(b, _):
+        for k in range(4):
+            one(4 * b + k, 0)
+        extra(2 * b, 0)
+        extra(2 * b + 1, 0)
+        return 0
+
+    lax.fori_loop(lo // 2, hi // 2, step, 0)
+
+
 def rounded(x):
     return x.astype(BF16).astype(F32)
 
@@ -66,10 +77,10 @@
 
 def kernel(
     fl, cl, fcnt, bcnt,
-    fpos, fvel, fmass, clv, bpos, bvel, brad, bmass, cid, hist,
+    fpos, fvel, fmass, bpos, bvel, brad, bmass, cid, hist,
     o_fa, o_fd, o_ba, o_h,
     hf, hb, hd, ut, qh, ql, stg, tf, tb, gb, ft, fi, hp, sc, ga, sp, cp, ry, red, rx,
-    cnf, cnb, dens, dr, pf, pu, ssem, rsem,
+    idc, cnf, cnb, dens, dr, pf, pu, ssem, rsem,
     *, n_x, n_y,
 ):
     me_x = lax.axis_index("gx")
@@ -87,9 +98,9 @@
     lane = lax.broadcasted_iota(jnp.int32, (32, 128), 1)
 
     for b in range(32):
-        cnf[b : b + 1, :] = jnp.full((1, 128), fcnt[b], jnp.int32)
+        cnf[b : b + 1, :] = jnp.full((1, 128), fcnt[0, 0, b], jnp.int32)
     for b in range(16):
-        cnb[b : b + 1, :] = jnp.full((1, 128), bcnt[b], jnp.int32)
+        cnb[b : b + 1, :] = jnp.full((1, 128), bcnt[0, 0, b], jnp.int32)
     f_on = lane < cnf[...]
     b_on = lane[:16] < cnb[...]
     hf[4, 0] = jnp.where(f_on, jnp.exp(jnp.log(fmass[...]) * (1.0 / 3.0)), 0.0)
@@ -126,6 +137,9 @@
     c_ym = copy(cp.at[0], ry.at[1], 25, ym)
     c_xp = copy(red.at[2], rx.at[0], 26, xp)
     c_xm = copy(red.at[0], rx.at[1], 27, xm)
+
+    for e in range(128):
+        idc[e : e + 1, :] = jnp.full((1, 128), cl[0, 0, e // 4, e % 4], jnp.int32)
 
     one1 = jnp.ones((1, 128), F32)
     zeros = lambda n: jnp.zeros((n, 128), F32)
@@ -218,9 +232,6 @@
                 hp[pl.ds(t * 128 + half * 4 + w, 16, stride=8), :] = words[w]
 
     def gather(tiles, first):
-        for t in tiles:
-            pack(t)
-
         def block(b, _):
             st = pl.multiple_of(b * 128, 128)
             ids8 = cid[:, pl.ds(st, 128)]
@@ -247,7 +258,7 @@
                 ga[at, :] = out
             return 0
 
-        lax.fori_loop(0, 16, block, 0)
+        return block
 
     fluid_table(4)
     boulder_table(4)
@@ -255,7 +266,8 @@
     cf[5].wait_recv()
     fluid_table(3)
     fluid_table(5)
-    gather((4,), True)
+    pack(4)
+    lax.fori_loop(0, 16, gather((4,), True), 0)
 
     for k in (1, 7):
         cf[k].wait_recv()
@@ -277,7 +289,7 @@
         lhs = ut[i][:, 0:48]
         acc = jnp.zeros((128, 128), F32)
         for jj in range(4):
-            t2 = jnp.concatenate([tf[fl[i * 8 + jj * 2]], tf[fl[i * 8 + jj * 2 + 1]]], axis=1)
+            t2 = jnp.concatenate([tf[fl[0, 0, i, jj * 2]], tf[fl[0, 0, i, jj * 2 + 1]]], axis=1)
             u = jnp.maximum(dot(lhs, jnp.concatenate([t2, t2, t2], axis=0), NN), 0.0)
             sq = u * u
             cube = sq * u
@@ -294,12 +306,15 @@
         dens[pl.ds(i, 1), :] = total[0:1]
         return 0
 
-    paired(0, 16, density)
+    pack(3)
+    pack(5)
+    side = gather((3, 5), False)
+    beside(0, 8, density, side)
     for k in (1, 7):
         cb[k].wait_recv()
     for k in (0, 2, 6, 8):
         cb[k].start()
-    paired(16, 32, density)
+    beside(8, 16, density, side)
     rho = fmass[...] + dens[...]
     hd[4] = STIFF * (rho / REST - 1.0) / (rho * rho)
     for k in (1, 7, 3, 5):
@@ -317,7 +332,7 @@
         fside = fi[pl.ds(pl.multiple_of(i * 8, 8), 8), :].astype(BF16)
         pulled = jnp.zeros((16, 128), F32)
         for h in range(2):
-            n0, n1 = cl[i * 4 + 2 * h], cl[i * 4 + 2 * h + 1]
+            n0, n1 = cl[0, 0, i, 2 * h], cl[0, 0, i, 2 * h + 1]
             t2 = jnp.concatenate([tb[n0], tb[n1]], axis=1)
             u = jnp.maximum(dot(lhs, jnp.concatenate([t2, t2, t2], axis=0), NN), 0.0)
             hi, lo = halves(u * u)
@@ -332,15 +347,19 @@
             dr[r, pl.ds(i, 1), :] = d4[r : r + 1]
         return 0
 
-    paired(0, 20, coupling)
+    for t in (1, 7, 0, 2, 6, 8):
+        pack(t)
+    side = gather((1, 7, 0), False)
+    beside(0, 10, coupling, side)
     for k in (1, 7):
         cd[k].wait_recv()
     for k in (0, 2, 6, 8):
         cd[k].start()
-    paired(20, 32, coupling)
+    beside(10, 16, coupling, side)
 
     onehot = (
-        lax.broadcasted_iota(jnp.int32, (144, 128), 0) == jnp.broadcast_to(clv[...], (144, 128))
+        lax.broadcasted_iota(jnp.int32, (144, 128), 0)
+        == jnp.broadcast_to(idc[...].T[0:1], (144, 128))
     ).astype(F32).astype(BF16)
 
     def reduced(r):
@@ -377,7 +396,7 @@
         press_table(k)
 
     def pressure(i, _):
-        fun = jnp.concatenate([ft[fl[i * 8 + j]] for j in range(8)], axis=1)
+        fun = jnp.concatenate([ft[fl[0, 0, i, j]] for j in range(8)], axis=1)
         got = dot(fun, qh[i], NT) + dot(fun, ql[i], NT)
         p8 = got[0:8] + got[8:16]
         at = pl.ds(i, 1)
@@ -387,21 +406,19 @@
             pf[d, at, :] = (fpos[d, at, :] - 0.5) * comb[0] - comb[d + 1]
         return 0
 
-    paired(0, 16, pressure)
+    side = gather((2, 6, 8), False)
+    beside(0, 8, pressure, side)
     c_yp.wait_recv()
     c_ym.wait_recv()
     for g in range(3):
         red[g] = cp[1, g] + (ry[0, g] + ry[1, g])
     c_xp.start()
     c_xm.start()
-    paired(16, 32, pressure)
+    beside(8, 16, pressure, side)
     for d in range(3):
         down = -1.0 if d == 2 else 0.0
         drag = dr[1 + d] - fvel[d] * dr[0]
         o_fa[d] = jnp.where(f_on, PRESS_C * pf[d] + drag + down, 0.0)
-
-    gather((3, 5, 1, 7), False)
-    gather((0, 2, 6, 8), False)
 
     def contact(b, _):
         st = pl.multiple_of(b * 128, 128)
@@ -477,7 +494,7 @@
             jax.ShapeDtypeStruct((3, 16, 128), F32),
             jax.ShapeDtypeStruct((3, 8, 2048), F32),
         ),
-        in_specs=[sm] * 4 + [vm] * 10,
+        in_specs=[sm] * 4 + [vm] * 9,
         out_specs=(vm,) * 4,
         scratch_shapes=[
             pltpu.VMEM((9, 4, 32, 128), F32),
@@ -500,6 +517,7 @@
             pltpu.VMEM((2, 3, 3, 16, 128), F32),
             pltpu.VMEM((3, 3, 16, 128), F32),
             pltpu.VMEM((2, 3, 16, 128), F32),
+            pltpu.VMEM((128, 128), jnp.int32),
             pltpu.VMEM((32, 128), jnp.int32),
             pltpu.VMEM((16, 128), jnp.int32),
             pltpu.VMEM((32, 128), F32),
@@ -513,14 +531,13 @@
             collective_id=0, has_side_effects=True, vmem_limit_bytes=67043328
         ),
     )(
-        fluid_lists.reshape(256),
-        coupling_lists.reshape(128),
-        fluid_counts.reshape(32),
-        boulder_counts.reshape(16),
+        fluid_lists,
+        coupling_lists,
+        fluid_counts,
+        boulder_counts,
         fluid_position.reshape(3, 32, 128),
         fluid_velocity.reshape(3, 32, 128),
         fluid_mass.reshape(32, 128),
-        coupling_lists.reshape(1, 128),
         boulder_position.reshape(3, 16, 128),
         boulder_velocity.reshape(3, 16, 128),
         boulder_radius.reshape(16, 128),

time: 80 us -> 70.8 us (0.89)
  Pallas kernels: 71.8 us -> 63.4 us
    pallas_call x1, Pallas kernels: 71.8 us -> 63.4 us  [body(): pl.pallas_call(lambda *refs: kernel(*refs, n_x=n_x, n_y=n_y), name='step'...]
    reshape x3 -> x0, local copies, waits for them, and re-layouts: 1.89 us -> none  [the longest x1 0.65 us: body(): fluid_lists.reshape(256)]
    unnamed x14, local copies, waits for them, and re-layouts: 5.3 us -> 6.45 us
where the time goes in v4:
time: 70.8 us; the launch traced here: 70.5 us
  Pallas kernels  63.4 us (90%)
  local copies, waits for them, and re-layouts  6.45 us (9%)
    pallas_call x1, Pallas kernels, body(): pl.pallas_call(lambda *refs: kernel(*refs, n_x=n_x, n_y=n_y), name='step'...  63.4 us
    unnamed x14, local copies, waits for them, and re-layouts  6.45 us

profile of v4, /device:TPU:1, one launch (start us, length us, event | category | flops | bytes accessed | tf_op | source)
XLA Modules:
  0.0 70.5 jit_solution(18176970863493093936)
XLA Ops:
  0.6 0.0 copy-start.2
  0.6 0.7 copy-done.2
  1.3 0.0 copy-start.3
  1.3 0.7 copy.22.refs_0_
  2.0 0.0 copy-done.3
  2.0 0.7 copy.23.refs_1_
  2.7 63.4 %step.1 = (f32[3,32,128]{2,1,0:T(8,128)}, f32[32,128]{1,0:T(8,128)}, f32[3,16,128]{2,1,0:T(8,128)}, f32[3,8,2048]{2,1,0:T(8,128)}) custom-call(s32[1,1,32,8]{3,2,1,0:T(8,128)} %copy.22.refs_0_, s32[1,1,32,4]{3,2,1,0:T(8,128)} %copy.23.refs_1_, s32[1,1,32]{2,1,0:T(1,128)} %refs_2_.1, s32[1,1,16]{2,1,0:T(1,128)} %refs_3_.1, f32[3,32,128]{2,1,0:T(8,128)} %bitcast.18, ...), custom_call_target="tpu_custom_call" | custom-call | tf_op jit(solution)/shard_map/step/pallas_call | solution.py:488
  66.1 0.0 copy-start.1
  66.1 1.4 %copy.31 = f32[3,1,1,4096]{3,2,1,0:T(1,128)} copy(f32[3,1,1,4096]{3,2,1,0:T(1,128)} %bitcast.20) | data formatting | bytes 98304
  67.5 0.0 copy-done.1
  67.5 0.0 copy-start
  67.5 0.6 copy.32
  68.1 0.1 copy-done
  68.3 0.6 copy.33
  68.9 1.6 %copy.34 = f32[3,1,1,8,2048]{4,3,2,1,0:T(8,128)} copy(f32[3,1,1,8,2048]{4,3,2,1,0:T(8,128)} %bitcast.15) | data formatting | bytes 393216
Async XLA Ops:
  0.6 0.7 copy-start.2
  1.3 0.7 copy-start.3
  66.1 1.4 %copy-start.1 = (f32[32,128]{1,0:T(8,128)S(1)}, f32[32,128]{1,0:T(8,128)}, u32[]{:S(2)}) copy-start(f32[32,128]{1,0:T(8,128)} %get-tuple-element.9) | copy-start | bytes 49156
  67.5 0.7 %copy-start = (f32[3,16,128]{2,1,0:T(8,128)S(1)}, f32[3,16,128]{2,1,0:T(8,128)}, u32[]{:S(2)}) copy-start(f32[3,16,128]{2,1,0:T(8,128)} %get-tuple-element.10) | copy-start | bytes 73732

commit v5 on v4

--- a/solution.py
+++ b/solution.py
@@ -77,10 +77,10 @@
 
 def kernel(
     fl, cl, fcnt, bcnt,
-    fpos, fvel, fmass, bpos, bvel, brad, bmass, cid, hist,
-    o_fa, o_fd, o_ba, o_h,
-    hf, hb, hd, ut, qh, ql, stg, tf, tb, gb, ft, fi, hp, sc, ga, sp, cp, ry, red, rx,
-    idc, cnf, cnb, dens, dr, pf, pu, ssem, rsem,
+    fpos, fvel, fmass, bpos, bvel, brad, bmass, cid,
+    o_fa, o_fd, ga, sc, o_cp,
+    hf, hb, hd, ut, qh, ql, stg, tf, tb, gb, ft, fi, hp, sp, cp, ry, red, rx,
+    idc, cnf, cnb, dens, dr, pf, ssem, rsem,
     *, n_x, n_y,
 ):
     me_x = lax.axis_index("gx")
@@ -297,12 +297,8 @@
             at = slice(jj * 256, (jj + 1) * 256)
             qh[i, :, at] = sq.astype(BF16)
             ql[i, :, at] = (sq - qh[i, :, at].astype(F32)).astype(BF16)
-        a, b, c = split3(acc)
-        total = (
-            dot(ones8, a.astype(BF16), NT)
-            + dot(ones8, b.astype(BF16), NT)
-            + dot(ones8, c.astype(BF16), NT)
-        )
+        a, b = halves(acc)
+        total = dot(ones8, a, NT) + dot(ones8, b, NT)
         dens[pl.ds(i, 1), :] = total[0:1]
         return 0
 
@@ -419,6 +415,28 @@
         down = -1.0 if d == 2 else 0.0
         drag = dr[1 + d] - fvel[d] * dr[0]
         o_fa[d] = jnp.where(f_on, PRESS_C * pf[d] + drag + down, 0.0)
+
+    c_xp.wait_recv()
+    c_xm.wait_recv()
+    for d in range(3):
+        o_cp[d] = red[1, d] + (rx[0, d] + rx[1, d])
+
+    for group in (cf, cb, cd):
+        for k in group:
+            group[k].wait_send()
+    for c in (c_yp, c_ym, c_xp, c_xm):
+        c.wait_send()
+
+
+def contact_kernel(
+    bcnt, bpos, bvel, brad, bmass, cid, hist, ga, sc, coupled, fa, fd,
+    o_fa, o_fd, o_ba, o_h, cnb, pu,
+):
+    o_fa[...] = fa[...]
+    o_fd[...] = fd[...]
+    for b in range(16):
+        cnb[b : b + 1, :] = jnp.full((1, 128), bcnt[0, 0, b], jnp.int32)
+    b_on = lax.broadcasted_iota(jnp.int32, (16, 128), 1) < cnb[...]
 
     def contact(b, _):
         st = pl.multiple_of(b * 128, 128)
@@ -463,18 +481,9 @@
 
     lax.fori_loop(0, 16, contact, 0)
 
-    c_xp.wait_recv()
-    c_xm.wait_recv()
     for d in range(3):
         down = -1.0 if d == 2 else 0.0
-        coupled = red[1, d] + (rx[0, d] + rx[1, d])
-        o_ba[d] = jnp.where(b_on, (pu[d] + coupled) / bmass[...] + down, 0.0)
-
-    for group in (cf, cb, cd):
-        for k in group:
-            group[k].wait_send()
-    for c in (c_yp, c_ym, c_xp, c_xm):
-        c.wait_send()
+        o_ba[d] = jnp.where(b_on, (pu[d] + coupled[d]) / bmass[...] + down, 0.0)
 
 
 def body(
@@ -485,17 +494,23 @@
     n_x, n_y = lax.axis_size("gx"), lax.axis_size("gy")
     vm = pl.BlockSpec(memory_space=pltpu.VMEM)
     sm = pl.BlockSpec(memory_space=pltpu.SMEM)
-    outs = pl.pallas_call(
+    pos_b = boulder_position.reshape(3, 16, 128)
+    vel_b = boulder_velocity.reshape(3, 16, 128)
+    rad_b = boulder_radius.reshape(16, 128)
+    mass_b = boulder_mass.reshape(16, 128)
+    ids = contact_ids.reshape(8, 2048)
+    fa, fd, words, scales, coupled = pl.pallas_call(
         lambda *refs: kernel(*refs, n_x=n_x, n_y=n_y),
         name="step",
         out_shape=(
             jax.ShapeDtypeStruct((3, 32, 128), F32),
             jax.ShapeDtypeStruct((32, 128), F32),
+            jax.ShapeDtypeStruct((512, 128), jnp.int32),
+            jax.ShapeDtypeStruct((9, 8, 128), F32),
             jax.ShapeDtypeStruct((3, 16, 128), F32),
-            jax.ShapeDtypeStruct((3, 8, 2048), F32),
         ),
-        in_specs=[sm] * 4 + [vm] * 9,
-        out_specs=(vm,) * 4,
+        in_specs=[sm] * 4 + [vm] * 8,
+        out_specs=(vm,) * 5,
         scratch_shapes=[
             pltpu.VMEM((9, 4, 32, 128), F32),
             pltpu.VMEM((9, 8, 16, 128), F32),
@@ -510,8 +525,6 @@
             pltpu.VMEM((288, 16, 128), BF16),
             pltpu.VMEM((256, 128), F32),
             pltpu.VMEM((1152, 128), jnp.int32),
-            pltpu.VMEM((9, 8, 128), F32),
-            pltpu.VMEM((512, 128), jnp.int32),
             pltpu.VMEM((1024, 128), F32),
             pltpu.VMEM((3, 3, 3, 16, 128), F32),
             pltpu.VMEM((2, 3, 3, 16, 128), F32),
@@ -523,7 +536,6 @@
             pltpu.VMEM((32, 128), F32),
             pltpu.VMEM((4, 32, 128), F32),
             pltpu.VMEM((3, 32, 128), F32),
-            pltpu.VMEM((3, 16, 128), F32),
             pltpu.SemaphoreType.DMA((28,)),
             pltpu.SemaphoreType.DMA((28,)),
         ],
@@ -538,14 +550,29 @@
         fluid_position.reshape(3, 32, 128),
         fluid_velocity.reshape(3, 32, 128),
         fluid_mass.reshape(32, 128),
-        boulder_position.reshape(3, 16, 128),
-        boulder_velocity.reshape(3, 16, 128),
-        boulder_radius.reshape(16, 128),
-        boulder_mass.reshape(16, 128),
-        contact_ids.reshape(8, 2048),
-        spring_history.reshape(3, 8, 2048),
+        pos_b,
+        vel_b,
+        rad_b,
+        mass_b,
+        ids,
     )
-    fa, fd, ba, ho = outs
+    fa, fd, ba, ho = pl.pallas_call(
+        contact_kernel,
+        name="contact",
+        out_shape=(
+            jax.ShapeDtypeStruct((3, 32, 128), F32),
+            jax.ShapeDtypeStruct((32, 128), F32),
+            jax.ShapeDtypeStruct((3, 16, 128), F32),
+            jax.ShapeDtypeStruct((3, 8, 2048), F32),
+        ),
+        in_specs=[sm] + [vm] * 11,
+        out_specs=(vm,) * 4,
+        scratch_shapes=[pltpu.VMEM((16, 128), jnp.int32), pltpu.VMEM((3, 16, 128), F32)],
+        compiler_params=pltpu.CompilerParams(vmem_limit_bytes=67043328),
+    )(
+        boulder_counts, pos_b, vel_b, rad_b, mass_b, ids,
+        spring_history.reshape(3, 8, 2048), words, scales, coupled, fa, fd,
+    )
     return (
         fa.reshape(3, 1, 1, 4096),
         fd.reshape(1, 1, 4096),

time: 70.8 us -> 68.9 us (0.973)
  local copies, waits for them, and re-layouts: 6.45 us -> 2.05 us
  Pallas kernels: 63.4 us -> 66 us
    unnamed x14 -> x6, local copies, waits for them, and re-layouts: 6.45 us -> 2.05 us
    pallas_call x0 -> x1, Pallas kernels: none -> 2.69 us  [body(): pl.pallas_call(contact_kernel, name='contact', out_shape=(jax.ShapeDtypeS...]
where the time goes in v5:
time: 68.9 us; the launch traced here: 68.7 us
  Pallas kernels  66 us (96%)
  local copies, waits for them, and re-layouts  2.05 us (3%)
    pallas_call x1, Pallas kernels, body(): pl.pallas_call(lambda *refs: kernel(*refs, n_x=n_x, n_y=n_y), name='step'...  63.3 us
    pallas_call x1, Pallas kernels, body(): pl.pallas_call(contact_kernel, name='contact', out_shape=(jax.ShapeDtypeS...  2.69 us
    unnamed x6, local copies, waits for them, and re-layouts  2.05 us

profile of v5, /device:TPU:1, one launch (start us, length us, event | category | flops | bytes accessed | tf_op | source)
XLA Modules:
  0.0 68.7 jit_solution(4565928735230803513)
XLA Ops:
  0.6 0.0 copy-start
  0.6 0.7 copy-done
  1.3 0.0 copy-start.1
  1.3 0.7 copy.22.refs_0_
  2.0 0.0 copy-done.1
  2.0 0.7 %copy.23.refs_1_ = s32[1,1,32,4]{3,2,1,0:T(8,128)} copy(s32[1,1,32,4]{2,3,1,0:T(4,128)S(1)} %copy-done.1) | data formatting | bytes 1024 | tf_op args[5]
  2.7 63.3 %step.1 = (f32[3,32,128]{2,1,0:T(8,128)}, f32[32,128]{1,0:T(8,128)}, s32[512,128]{1,0:T(8,128)}, f32[9,8,128]{2,1,0:T(8,128)}, f32[3,16,128]{2,1,0:T(8,128)}) custom-call(s32[1,1,32,8]{3,2,1,0:T(8,128)} %copy.22.refs_0_, s32[1,1,32,4]{3,2,1,0:T(8,128)} %copy.23.refs_1_, s32[1,1,32]{2,1,0:T(1,128)} %refs_2_.1, s32[1,1,16]{2,1,0:T(1,128)} %bcnt.1, ...), custom_call_target="tpu_custom_call" | custom-call | tf_op jit(solution)/shard_map/step/pallas_call | solution.py:502
  66.0 2.7 %contact.1 = (f32[3,32,128]{2,1,0:T(8,128)}, f32[32,128]{1,0:T(8,128)}, f32[3,16,128]{2,1,0:T(8,128)}, f32[3,8,2048]{2,1,0:T(8,128)}) custom-call(s32[1,1,16]{2,1,0:T(1,128)} %bcnt.1, f32[3,16,128]{2,1,0:T(8,128)} %bitcast.19, f32[3,16,128]{2,1,0:T(8,128)} %bitcast.21, f32[16,128]{1,0:T(8,128)} %bitcast.25, f32[16,128]{1,0:T(8,128)} %bitcast.27, ...), custom_call_target="tpu_custom_call" | custom-call | tf_op jit(solution)/shard_map/contact/pallas_call | solution.py:559
Async XLA Ops:
  0.6 0.7 %copy-start = (s32[1,1,32,8]{2,3,1,0:T(8,128)S(1)}, s32[1,1,32,8]{2,3,1,0:T(8,128)}, u32[]{:S(2)}) copy-start(s32[1,1,32,8]{2,3,1,0:T(8,128)} %param.17) | copy-start | bytes 3076
  1.3 0.7 copy-start.1
